TPU v7x, 256 devices: a whole 4x4x8 slice. The times are simulated.
256 devices in a mesh: src: 16 (over z_lo, y), tgt: 16 (over x, z_hi, core).
Axes of the slice: x: 4, y: 4, z: 8 (z_hi: 2, z_lo: 4; z = z_hi * 4 + z_lo), core: 2. Of those that a mesh axis runs over, the one named last changes fastest.
Arguments:
- coefficients: bfloat16 [65536, 16, 128], P(('src', 'tgt')), may hold values from -6 to 6
- phases: float32 [8, 65536, 64], P(None, ('src', 'tgt')), may hold values from -3.140625 to 3.140625
- classes: int32 [8, 65536], P(None, ('src', 'tgt')), may hold values from 0 to 1
- blocks: bfloat16 [8, 2, 2, 128, 256], replicated, may hold values from -0.375 to 0.375
- evaluation: bfloat16 [128, 128], replicated, may hold values from -0.125 to 0.125
Outputs:
- target_values: bfloat16 [16, 256, 16, 128], P('tgt', 'src')
All inputs are finite; a program needn't handle non-finite values.
Results may differ from a plain program's by a relative error of at most 0.029.
Values may be sent and summed in bfloat16 or wider, within the bound.
A program may use at most 64 MiB of HBM per device.

v0:
```python
import jax
import jax.numpy as jnp
from jax import lax
from jax.sharding import PartitionSpec as P

LEVELS = 8


def swapped(block, axis, distance):
    count = lax.axis_size(axis)
    route = []
    for low in range(count):
        high = low | 1 << distance
        if high != low and high < count:
            route += [(low, high), (high, low)]
    return lax.ppermute(block, axis, route)


def rotate_phase(values, angles):
    half = angles.shape[-1]
    cosine = jnp.cos(angles)[:, None, :]
    sine = jnp.sin(angles)[:, None, :]
    real_part = values[..., :half]
    imag_part = values[..., half:]
    return jnp.concatenate(
        [cosine * real_part - sine * imag_part, sine * real_part + cosine * imag_part], axis=-1
    )


def contribute(current, kinds, columns):
    products = jnp.einsum("nkc,qcd->nqkd", current, columns, preferred_element_type=jnp.float32)
    chooser = (kinds[:, None] == jnp.arange(columns.shape[0], dtype=jnp.int32)[None, :]).astype(
        jnp.float32
    )
    return jnp.sum(products * chooser[:, :, None, None], axis=1)


def swap_partial(values, on_src, bit_pos):
    if on_src:
        return swapped(values.astype(jnp.bfloat16), "src", bit_pos).astype(values.dtype)
    return swapped(values.astype(jnp.bfloat16), "tgt", bit_pos).astype(values.dtype)


def per_device(coefficients, phases, classes, blocks, evaluation):
    current = coefficients
    width = current.shape[2]
    for level in range(LEVELS):
        on_src = level % 2 == 0
        if on_src:
            bit_pos = level // 2 % (lax.axis_size("src").bit_length() - 1)
            my_side = lax.axis_index("src") // 2**bit_pos % 2
        else:
            bit_pos = level // 2 % (lax.axis_size("tgt").bit_length() - 1)
            my_side = lax.axis_index("tgt") // 2**bit_pos % 2
        level_table = blocks[level]
        kinds = classes[level]
        angles = phases[level]
        own_table = lax.dynamic_index_in_dim(level_table, my_side, axis=1, keepdims=False)
        products = contribute(current, kinds, own_table)
        kept = lax.dynamic_slice_in_dim(products, my_side * width, width, 2)
        outgoing = lax.dynamic_slice_in_dim(products, (1 - my_side) * width, width, 2)
        arrived = swap_partial(outgoing, on_src, bit_pos)
        summed = kept + arrived
        current = rotate_phase(summed, angles).astype(jnp.bfloat16)
    shares = lax.psum_scatter(
        jnp.einsum("nkc,cd->nkd", current, evaluation, preferred_element_type=jnp.float32).astype(
            jnp.bfloat16
        ),
        "src",
        scatter_dimension=0,
        tiled=True,
    ).astype(jnp.float32)
    return shares[None].astype(jnp.bfloat16)


def solution(mesh):
    placed = (
        P(("src", "tgt"), None, None),
        P(None, ("src", "tgt"), None),
        P(None, ("src", "tgt")),
        P(),
        P(),
    )
    return jax.shard_map(
        per_device,
        mesh=mesh,
        in_specs=placed,
        out_specs=P("tgt", "src", None, None),
        check_vma=False,
    )
```

profile of v0, /device:TPU:4, one launch (start us, length us, event | category | flops | bytes accessed | tf_op | source)
XLA Modules:
  0.0 385.9 jit_solution(7421756104188266220)
XLA Ops:
  6.5 2.8 fusion.60
  15.7 3.2 constant_dynamic-slice_fusion.15
  20.8 3.5 cosine_bitcast_fusion.7
  27.4 11.8 %collective-permute-done = bf16[256,16,128]{2,0,1:T(8,128)(2,1)S(1)} collective-permute-done((bf16[256,16,128]{2,0,1:T(8,128)(2,1)}, bf16[256,16,128]{2,0,1:T(8,128)(2,1)S(1)}, u32[]{:S(2)}, u32[]{:S(2)}) %collective-permute-start) | collective-permute-done | bytes 1048608 | tf_op jit(solution)/shard_map/ppermute | solution.py:16
  46.7 3.2 constant_dynamic-slice_fusion.13
  55.1 2.0 copy-done.7
  58.6 3.2 collective-permute-start.2
  63.3 3.2 constant_dynamic-slice_fusion.11
  68.4 17.5 %collective-permute-done.2 = bf16[256,16,128]{2,0,1:T(8,128)(2,1)S(1)} collective-permute-done((bf16[256,16,128]{2,0,1:T(8,128)(2,1)}, bf16[256,16,128]{2,0,1:T(8,128)(2,1)S(1)}, u32[]{:S(2)}, u32[]{:S(2)}) %collective-permute-start.2) | collective-permute-done | bytes 1048608 | tf_op jit(solution)/shard_map/ppermute | solution.py:16
  88.4 2.0 copy-done.4
  91.8 7.2 %collective-permute-start.3 = (bf16[256,16,128]{2,0,1:T(8,128)(2,1)}, bf16[256,16,128]{2,0,1:T(8,128)(2,1)S(1)}, u32[]{:S(2)}, u32[]{:S(2)}) collective-permute-start(bf16[256,16,128]{2,0,1:T(8,128)(2,1)} %copy.89), channel_id=1, source_target_pairs={{0,2},{2,0},{1,3},{3,1},{4,6},{6,4},{5,7},{7,5},{8,10},{10,8},{9,1... | collective-permute-start | bytes 3145736 | tf_op jit(solution)/shard_map/ppermute | solution.py:16
  100.5 3.2 constant_dynamic-slice_fusion.9
  105.6 37.9 %collective-permute-done.3 = bf16[256,16,128]{2,0,1:T(8,128)(2,1)S(1)} collective-permute-done((bf16[256,16,128]{2,0,1:T(8,128)(2,1)}, bf16[256,16,128]{2,0,1:T(8,128)(2,1)S(1)}, u32[]{:S(2)}, u32[]{:S(2)}) %collective-permute-start.3) | collective-permute-done | bytes 1048608 | tf_op jit(solution)/shard_map/ppermute | solution.py:16
  149.5 2.4 collective-permute-start.4
  153.4 3.2 constant_dynamic-slice_fusion.7
  158.5 15.8 %collective-permute-done.4 = bf16[256,16,128]{2,0,1:T(8,128)(2,1)S(1)} collective-permute-done((bf16[256,16,128]{2,0,1:T(8,128)(2,1)}, bf16[256,16,128]{2,0,1:T(8,128)(2,1)S(1)}, u32[]{:S(2)}, u32[]{:S(2)}) %collective-permute-start.4) | collective-permute-done | bytes 1048608 | tf_op jit(solution)/shard_map/ppermute | solution.py:16
  183.1 3.2 constant_dynamic-slice_fusion.5
  188.2 15.8 %collective-permute-done.5 = bf16[256,16,128]{2,0,1:T(8,128)(2,1)S(1)} collective-permute-done((bf16[256,16,128]{2,0,1:T(8,128)(2,1)}, bf16[256,16,128]{2,0,1:T(8,128)(2,1)S(1)}, u32[]{:S(2)}, u32[]{:S(2)}) %collective-permute-start.5) | collective-permute-done | bytes 1048608 | tf_op jit(solution)/shard_map/ppermute | solution.py:16
  209.9 2.8 collective-permute-start.6
  214.2 3.2 constant_dynamic-slice_fusion.3
  219.3 36.9 %collective-permute-done.6 = bf16[256,16,128]{2,0,1:T(8,128)(2,1)S(1)} collective-permute-done((bf16[256,16,128]{2,0,1:T(8,128)(2,1)}, bf16[256,16,128]{2,0,1:T(8,128)(2,1)S(1)}, u32[]{:S(2)}, u32[]{:S(2)}) %collective-permute-start.6) | collective-permute-done | bytes 1048608 | tf_op jit(solution)/shard_map/ppermute | solution.py:16
  262.7 3.2 constant_dynamic-slice_fusion.1
  267.8 20.5 %collective-permute-done.7 = bf16[256,16,128]{2,0,1:T(8,128)(2,1)S(1)} collective-permute-done((bf16[256,16,128]{2,0,1:T(8,128)(2,1)}, bf16[256,16,128]{2,0,1:T(8,128)(2,1)S(1)}, u32[]{:S(2)}, u32[]{:S(2)}) %collective-permute-start.7) | collective-permute-done | bytes 1048608 | tf_op jit(solution)/shard_map/ppermute | solution.py:16
  291.0 86.5 %reduce-scatter.2.cloned.1.call-done = bf16[16,16,128]{2,0,1:T(8,128)(2,1)} async-done(((bf16[256,16,128]{2,0,1:T(8,128)(2,1)}), bf16[16,16,128]{2,0,1:T(8,128)(2,1)}) %reduce-scatter.2.cloned.1.call-update) | async-done | bytes 65552 | tf_op jit(solution)/shard_map/reduce_scatter | solution.py:65
  (168 shorter events, 77.9 us)
Async XLA Ops:
  6.5 282.8 %copy-start = (bf16[128,128]{1,0:T(8,128)(2,1)S(1)}, bf16[128,128]{1,0:T(8,128)(2,1)}, u32[]{:S(2)}) copy-start(bf16[128,128]{1,0:T(8,128)(2,1)} %param.9) | copy-start | bytes 98308
  6.5 371.0 %reduce-scatter.2.cloned.1.call-start = ((), (), s32[]{:S(2)}) async-start(), calls=%async_computation.1 | async-start | bytes 1114112 | tf_op jit(solution)/shard_map/reduce_scatter | solution.py:65
  14.1 25.1 %collective-permute-start = (bf16[256,16,128]{2,0,1:T(8,128)(2,1)}, bf16[256,16,128]{2,0,1:T(8,128)(2,1)S(1)}, u32[]{:S(2)}, u32[]{:S(2)}) collective-permute-start(bf16[256,16,128]{2,0,1:T(8,128)(2,1)} %copy.83), channel_id=1, source_target_pairs={{0,16},{16,0},{32,48},{48,32},{64,80},{80,64},{96,112},{112,96},{1... | collective-permute-start | bytes 3145736 | tf_op jit(solution)/shard_map/ppermute | solution.py:16
  27.4 12.0 %copy-start.28 = (f32[256,64]{1,0:T(8,128)S(1)}, f32[256,64]{1,0:T(8,128)}, u32[]{:S(2)}) copy-start(f32[256,64]{1,0:T(8,128)} %copy.46) | copy-start | bytes 196612
  27.4 12.0 %copy-start.29 = (f32[256,64]{1,0:T(8,128)S(1)}, f32[256,64]{1,0:T(8,128)}, u32[]{:S(2)}) copy-start(f32[256,64]{1,0:T(8,128)} %copy.51) | copy-start | bytes 196612
  45.2 6.6 %collective-permute-start.1 = (bf16[256,16,128]{2,0,1:T(8,128)(2,1)}, bf16[256,16,128]{2,0,1:T(8,128)(2,1)S(1)}, u32[]{:S(2)}, u32[]{:S(2)}) collective-permute-start(bf16[256,16,128]{2,0,1:T(8,128)(2,1)} %copy.85), channel_id=1, source_target_pairs={{0,1},{1,0},{2,3},{3,2},{4,5},{5,4},{6,7},{7,6},{8,9},{9,8},{10,11... | collective-permute-start | bytes 3145736 | tf_op jit(solution)/shard_map/ppermute | solution.py:16
  58.6 27.3 %collective-permute-start.2 = (bf16[256,16,128]{2,0,1:T(8,128)(2,1)}, bf16[256,16,128]{2,0,1:T(8,128)(2,1)S(1)}, u32[]{:S(2)}, u32[]{:S(2)}) collective-permute-start(bf16[256,16,128]{2,0,1:T(8,128)(2,1)} %copy.87), channel_id=1, source_target_pairs={{0,32},{32,0},{16,48},{48,16},{64,96},{96,64},{80,112},{112,80},{1... | collective-permute-start | bytes 3145736 | tf_op jit(solution)/shard_map/ppermute | solution.py:16
  68.3 17.7 %copy-start.18 = (f32[256,64]{1,0:T(8,128)S(1)}, f32[256,64]{1,0:T(8,128)}, u32[]{:S(2)}) copy-start(f32[256,64]{1,0:T(8,128)} %copy.42) | copy-start | bytes 196612
  68.4 17.7 %copy-start.24 = (f32[256,64]{1,0:T(8,128)S(1)}, f32[256,64]{1,0:T(8,128)}, u32[]{:S(2)}) copy-start(f32[256,64]{1,0:T(8,128)} %copy.57) | copy-start | bytes 196612
  90.4 8.6 %copy-start.38 = (f32[256,64]{0,1:T(8,128)S(1)}, f32[256,64]{0,1:T(8,128)}, u32[]{:S(2)}) copy-start(f32[256,64]{0,1:T(8,128)} %get-tuple-element.39) | copy-start | bytes 196612
  90.4 9.4 %copy-start.37 = (f32[256,64]{0,1:T(8,128)S(1)}, f32[256,64]{0,1:T(8,128)}, u32[]{:S(2)}) copy-start(f32[256,64]{0,1:T(8,128)} %get-tuple-element.34) | copy-start | bytes 196612
  91.8 51.7 %collective-permute-start.3 = (bf16[256,16,128]{2,0,1:T(8,128)(2,1)}, bf16[256,16,128]{2,0,1:T(8,128)(2,1)S(1)}, u32[]{:S(2)}, u32[]{:S(2)}) collective-permute-start(bf16[256,16,128]{2,0,1:T(8,128)(2,1)} %copy.89), channel_id=1, source_target_pairs={{0,2},{2,0},{1,3},{3,1},{4,6},{6,4},{5,7},{7,5},{8,10},{10,8},{9,1... | collective-permute-start | bytes 3145736 | tf_op jit(solution)/shard_map/ppermute | solution.py:16
  105.6 38.2 %copy-start.19 = (f32[256,64]{1,0:T(8,128)S(1)}, f32[256,64]{1,0:T(8,128)}, u32[]{:S(2)}) copy-start(f32[256,64]{1,0:T(8,128)} %copy.40) | copy-start | bytes 196612
  105.6 38.2 %copy-start.25 = (f32[256,64]{1,0:T(8,128)S(1)}, f32[256,64]{1,0:T(8,128)}, u32[]{:S(2)}) copy-start(f32[256,64]{1,0:T(8,128)} %copy.60) | copy-start | bytes 196612
  149.5 24.8 %collective-permute-start.4 = (bf16[256,16,128]{2,0,1:T(8,128)(2,1)}, bf16[256,16,128]{2,0,1:T(8,128)(2,1)S(1)}, u32[]{:S(2)}, u32[]{:S(2)}) collective-permute-start(bf16[256,16,128]{2,0,1:T(8,128)(2,1)} %copy.91), channel_id=1, source_target_pairs={{0,64},{64,0},{16,80},{80,16},{32,96},{96,32},{48,112},{112,48},{1... | collective-permute-start | bytes 3145736 | tf_op jit(solution)/shard_map/ppermute | solution.py:16
  158.5 16.1 %copy-start.20 = (f32[256,64]{1,0:T(8,128)S(1)}, f32[256,64]{1,0:T(8,128)}, u32[]{:S(2)}) copy-start(f32[256,64]{1,0:T(8,128)} %copy.38) | copy-start | bytes 196612
  158.5 16.1 %copy-start.26 = (f32[256,64]{1,0:T(8,128)S(1)}, f32[256,64]{1,0:T(8,128)}, u32[]{:S(2)}) copy-start(f32[256,64]{1,0:T(8,128)} %copy.63) | copy-start | bytes 196612
  180.3 23.6 %collective-permute-start.5 = (bf16[256,16,128]{2,0,1:T(8,128)(2,1)}, bf16[256,16,128]{2,0,1:T(8,128)(2,1)S(1)}, u32[]{:S(2)}, u32[]{:S(2)}) collective-permute-start(bf16[256,16,128]{2,0,1:T(8,128)(2,1)} %copy.93), channel_id=1, source_target_pairs={{0,4},{4,0},{1,5},{5,1},{2,6},{6,2},{3,7},{7,3},{8,12},{12,8},{9,1... | collective-permute-start | bytes 3145736 | tf_op jit(solution)/shard_map/ppermute | solution.py:16
  188.1 16.0 %copy-start.21 = (f32[256,64]{1,0:T(8,128)S(1)}, f32[256,64]{1,0:T(8,128)}, u32[]{:S(2)}) copy-start(f32[256,64]{1,0:T(8,128)} %copy.36) | copy-start | bytes 196612
  188.2 16.0 %copy-start.27 = (f32[256,64]{1,0:T(8,128)S(1)}, f32[256,64]{1,0:T(8,128)}, u32[]{:S(2)}) copy-start(f32[256,64]{1,0:T(8,128)} %copy.66) | copy-start | bytes 196612
  209.9 46.3 %collective-permute-start.6 = (bf16[256,16,128]{2,0,1:T(8,128)(2,1)}, bf16[256,16,128]{2,0,1:T(8,128)(2,1)S(1)}, u32[]{:S(2)}, u32[]{:S(2)}) collective-permute-start(bf16[256,16,128]{2,0,1:T(8,128)(2,1)} %copy.95), channel_id=1, source_target_pairs={{0,128},{128,0},{16,144},{144,16},{32,160},{160,32},{48,176},{176,... | collective-permute-start | bytes 3145736 | tf_op jit(solution)/shard_map/ppermute | solution.py:16
  219.2 37.1 %copy-start.16 = (f32[256,64]{1,0:T(8,128)S(1)}, f32[256,64]{1,0:T(8,128)}, u32[]{:S(2)}) copy-start(f32[256,64]{1,0:T(8,128)} %copy.34) | copy-start | bytes 196612
  219.3 37.1 %copy-start.22 = (f32[256,64]{1,0:T(8,128)S(1)}, f32[256,64]{1,0:T(8,128)}, u32[]{:S(2)}) copy-start(f32[256,64]{1,0:T(8,128)} %copy.69) | copy-start | bytes 196612
  262.0 26.3 %collective-permute-start.7 = (bf16[256,16,128]{2,0,1:T(8,128)(2,1)}, bf16[256,16,128]{2,0,1:T(8,128)(2,1)S(1)}, u32[]{:S(2)}, u32[]{:S(2)}) collective-permute-start(bf16[256,16,128]{2,0,1:T(8,128)(2,1)} %copy.97), channel_id=1, source_target_pairs={{0,8},{8,0},{1,9},{9,1},{2,10},{10,2},{3,11},{11,3},{4,12},{12,4},... | collective-permute-start | bytes 3145736 | tf_op jit(solution)/shard_map/ppermute | solution.py:16
  (29 other events, 68.4 us)
Sparse Core Ops, SparseCore 0:
  291.2 86.3 reduce-scatter.1
where the time goes:
time: 387 us; the launch traced here: 386 us
  waiting for transfers between devices  243 us (63%)
  local copies, waits for them, and re-layouts  89.6 us (23%)
  starting transfers between devices  18.8 us (5%)
  between operations  14.1 us (4%)
  matrix products  12.6 us (3%)
  other arithmetic  7.91 us (2%)
    ppermute x8, waiting for transfers between devices, swapped(): return lax.ppermute(block, axis, route)  156 us
    reduce_scatter x1, waiting for transfers between devices, per_device(): lax.psum_scatter(jnp.einsum('nkc,cd->nkd', current, evaluation, preferred...  86.5 us
    unnamed x104, local copies, waits for them, and re-layouts  43.2 us
    dynamic_slice x8, local copies, waits for them, and re-layouts, per_device(): kept = lax.dynamic_slice_in_dim(products, my_side * width, width, 2)  25.3 us
    ppermute x8, starting transfers between devices, swapped(): return lax.ppermute(block, axis, route)  18.8 us
    dot_general x8, matrix products, contribute(): jnp.einsum('nkc,qcd->nqkd', current, columns, preferred_element_type=jnp....  10.9 us
    cos x9, local copies, waits for them, and re-layouts, rotate_phase(): cosine = jnp.cos(angles)[:, None, :]  9.62 us
  transfers between devices with their start and end apart: 9, of which 8 were waited for; matrix products, arithmetic and copies ran while one was open for 15% of the time, Pallas kernels for 0%

commit v1 on v0

v1 whole, which is shorter than its diff:
```python
import jax
import jax.numpy as jnp
from jax import lax
from jax.experimental import pallas as pl
from jax.experimental.pallas import tpu as pltpu
from jax.sharding import PartitionSpec as P

MESH = pl.DeviceIdType.MESH
SIN = (3.1415927410125732, -5.167712688446045, 2.5501604080200195, -0.5992423295974731,
       0.08208189159631729, -0.007275315932929516, 0.0003952804545406252)
COS = (1.0, -4.93480110168457, 4.058694839477539, -1.3351584672927856,
       0.23502980172634125, -0.025358984246850014, 0.0015939107397571206)
STEP = 10430.378350470453


def horner(coefs, v):
    acc = jnp.full_like(v, coefs[-1])
    for a in coefs[-2::-1]:
        acc = acc * v + a
    return acc


def sin_cos(k):
    u = k.astype(jnp.float32) * (1.0 / 32768.0)
    v = u * u
    return u * horner(SIN, v), horner(COS, v)


def high(w):
    return w >> 16


def low(w):
    return (w << 16) >> 16


def word(a, b):
    return (a << 16) | (b & 0xFFFF)


def both_halves(value, lane, first):
    other = pltpu.roll(value, 64, 1)
    return jnp.where((lane < 64) == first, value, other)


def tables(w_ref_value, lane, part, first):
    k = part(w_ref_value)
    sine, cosine = sin_cos(k)
    cosine = both_halves(cosine, lane, first)
    sine = both_halves(sine, lane, first)
    return cosine, jnp.where(lane < 64, -sine, sine)


def level(x0, x1, m0, m1, weights, rot0, rot1):
    g = x0.shape[0]
    shape = (g, 8, 16, 128)
    rows = g * 128

    def split(x, m):
        xf = x.astype(jnp.float32)
        one = xf * jnp.broadcast_to(m[:, :, None, :], shape)
        return (xf - one).astype(jnp.bfloat16).reshape(rows, 128), one.astype(jnp.bfloat16).reshape(rows, 128)

    a0, a1 = split(x0, m0)
    b0, b1 = split(x1, m1)
    lhs = jnp.concatenate([a0, b0, a1, b1], axis=1)
    s = jnp.dot(lhs, weights, preferred_element_type=jnp.float32)
    outs = []
    for half, (c, sn) in enumerate((rot0, rot1)):
        v = s[:, half * 128:(half + 1) * 128]
        r = pltpu.roll(v, 64, 1)
        c = jnp.broadcast_to(c[:, :, None, :], shape).reshape(rows, 128)
        sn = jnp.broadcast_to(sn[:, :, None, :], shape).reshape(rows, 128)
        outs.append((v * c + r * sn).reshape(shape))
    return outs


def kernel(coef, ph, cls, wts_hbm, ev, out,
           wts, aux, a_co, a_aux, b_send, b_co, b_aux, cs3, ms3, cs5, ms5, osend,
           wsem, loc, sa, ra, ra2, sb, rb, sb2, rb2, so, ro, lb):
    s = lax.axis_index("src")
    t = lax.axis_index("tgt")
    y, zl = s % 4, s // 4
    c, zh, x = t % 2, (t // 2) % 2, t // 4
    ys = [(y + d) % 4 for d in range(4)]
    xs = [(x + d) % 4 for d in range(4)]
    zls = [(zl + d) % 4 for d in range(4)]
    cs = [c, 1 - c]
    zhs = [zh, 1 - zh]

    def dev(dx=0, dy=0, dl=0, dh=0, dc=0):
        return zls[dl] * 4 + ys[dy], xs[dx] * 4 + zhs[dh] * 2 + cs[dc]

    yc_peers = [(dy, dc) for dy in (2, 1, 3, 0) for dc in (0, 1) if (dy, dc) != (0, 0)]
    xz_peers = [(dx, dh, dl) for dx in (2, 1, 3, 0) for dh in (1, 0) for dl in (2, 1, 3, 0) if (dx, dh, dl) != (0, 0, 0)]
    out_peers = [(dx, dh, dc) for dx in (2, 1, 3, 0) for dh in (1, 0) for dc in (0, 1) if (dx, dh, dc) != (0, 0, 0)]

    barrier = pltpu.get_barrier_semaphore()
    count = 0
    for dx, dh, dl in xz_peers:
        pl.semaphore_signal(barrier, inc=1, device_id=dev(dx=dx, dh=dh, dl=dl), device_id_type=MESH)
        count += 1
    for dx, dh, dc in out_peers:
        if dc == 1 and (dx, dh) != (0, 0):
            pl.semaphore_signal(barrier, inc=1, device_id=dev(dx=dx, dh=dh, dc=dc), device_id_type=MESH)
            count += 1
    for dy, dc in yc_peers:
        pl.semaphore_signal(barrier, inc=1, device_id=dev(dy=dy, dc=dc), device_id_type=MESH)
        count += 1

    wcopy = pltpu.make_async_copy(wts_hbm, wts, wsem)
    wcopy.start()

    zeros = jnp.zeros((120, 256), jnp.int32)
    kinds = jnp.concatenate([cls[...], zeros], axis=0).T[:, :64]

    def fixed(l):
        return jnp.round(ph[l] * STEP).astype(jnp.int32)

    q = [fixed(l) for l in range(8)]
    aux[:, 0, 0, :] = jnp.concatenate([word(q[0], q[1]), word(q[2], kinds)], axis=1)
    aux[:, 1, 0, :] = jnp.concatenate([word(q[3], q[4]), word(q[5], q[6])], axis=1)
    aux[:, 2, 0, :] = jnp.concatenate([word(q[7], kinds), jnp.zeros((256, 64), jnp.int32)], axis=1)
    aux_n = aux.reshape(4, 4, 4, 2, 2, 3, 1, 128)

    pl.semaphore_wait(barrier, count)

    me_yc = y * 2 + c
    chunks = [(dx, dh) for dx in (0, 2, 1, 3) for dh in (1, 0)]
    for k, (dx, dh) in enumerate(chunks):
        for dy, dc in yc_peers:
            to = dev(dy=dy, dc=dc)
            pltpu.make_async_remote_copy(
                aux_n.at[:, ys[dy], xs[dx], zhs[dh], cs[dc]], a_aux.at[k, me_yc], sa.at[0], ra2.at[k],
                device_id=to, device_id_type=MESH).start()
            pltpu.make_async_remote_copy(
                coef.at[:, ys[dy], xs[dx], zhs[dh], cs[dc]], a_co.at[k, me_yc], sa.at[1], ra.at[k],
                device_id=to, device_id_type=MESH).start()
        pltpu.make_async_copy(aux_n.at[:, y, xs[dx], zhs[dh], c], a_aux.at[k, me_yc], loc.at[k]).start()
        pltpu.make_async_copy(coef.at[:, y, xs[dx], zhs[dh], c], a_co.at[k, me_yc], loc.at[8 + k]).start()
    wcopy.wait()

    lane = lax.broadcasted_iota(jnp.int32, (8, 128), 1)

    def kind_rows(words, at):
        return jnp.broadcast_to(low(words)[:, at:at + 1], (8, 128)).astype(jnp.float32)

    me_slot = (xs[0] // 2, xs[0] % 2, zh, zl // 2, zl % 2)
    for k, (dx, dh) in enumerate(chunks):
        me = (s, t)
        pltpu.make_async_copy(aux_n.at[:, y, xs[dx], zhs[dh], c], a_aux.at[k, me_yc], loc.at[k]).wait()
        pltpu.make_async_copy(coef.at[:, y, xs[dx], zhs[dh], c], a_co.at[k, me_yc], loc.at[8 + k]).wait()
        pltpu.make_async_remote_copy(a_aux.at[k, pl.ds(0, 7)], a_aux.at[k, pl.ds(0, 7)], sa.at[0], ra2.at[k], device_id=me, device_id_type=MESH).wait_recv()
        pltpu.make_async_remote_copy(a_co.at[k, pl.ds(0, 7)], a_co.at[k, pl.ds(0, 7)], sa.at[1], ra.at[k], device_id=me, device_id_type=MESH).wait_recv()
        for dl in (2, 1, 3, 0):
            src = a_aux.at[k, :, zls[dl], pl.ds(1, 2)]
            if (dx, dh, dl) == (0, 0, 0):
                pltpu.make_async_copy(src, b_aux.at[me_slot], lb.at[0]).start()
            else:
                pltpu.make_async_remote_copy(src, b_aux.at[me_slot], sb2, rb2, device_id=dev(dx=dx, dh=dh, dl=dl), device_id_type=MESH).start()
        for n in range(4):
            w = a_aux[k, :, n, 0, 0, :]
            for l, (part, first) in enumerate(((high, True), (low, True), (high, False))):
                co, si = tables(w, lane, part, first)
                cs3[l, 0, n] = co
                cs3[l, 1, n] = si
                ms3[l, n] = kind_rows(w, 64 + l)
        cur = [a_co[k, b] for b in range(8)]
        for l, bit in enumerate((1, 0, 2)):
            step = 1 << bit
            lows = [b for b in range(8) if not b & step]

            def rows(table, chosen):
                return jnp.stack([table[:, b] for b in chosen], axis=1)

            highs = [b + step for b in lows]
            x0 = jnp.stack([cur[b] for b in lows], axis=1)
            x1 = jnp.stack([cur[b] for b in highs], axis=1)
            co, si, mm = cs3[l, 0], cs3[l, 1], ms3[l]
            shape = (4, 4, 16, 128)

            def split(v, m):
                vf = v.astype(jnp.float32)
                one = vf * jnp.broadcast_to(m[:, :, None, :], shape)
                return (vf - one).astype(jnp.bfloat16).reshape(256, 128), one.astype(jnp.bfloat16).reshape(256, 128)

            a0, a1 = split(x0, rows(mm, lows))
            b0, b1 = split(x1, rows(mm, highs))
            lhs = jnp.concatenate([a0, b0, a1, b1], axis=1)
            z = jnp.dot(lhs, wts[l], preferred_element_type=jnp.float32)
            nxt = [None] * 8
            for half, chosen in enumerate((lows, highs)):
                v = z[:, half * 128:(half + 1) * 128]
                r = pltpu.roll(v, 64, 1)
                cc = jnp.broadcast_to(rows(co, chosen)[:, :, None, :], shape).reshape(256, 128)
                ss = jnp.broadcast_to(rows(si, chosen)[:, :, None, :], shape).reshape(256, 128)
                o = (v * cc + r * ss).astype(jnp.bfloat16).reshape(shape)
                for j, b in enumerate(chosen):
                    nxt[b] = o[:, j]
            cur = nxt
        for b in range(8):
            b_send[k, :, b] = cur[b]
        for dl in (2, 1, 3, 0):
            src = b_send.at[k, zls[dl]]
            if (dx, dh, dl) == (0, 0, 0):
                pltpu.make_async_copy(src, b_co.at[me_slot], lb.at[1]).start()
            else:
                pltpu.make_async_remote_copy(src, b_co.at[me_slot], sb, rb, device_id=dev(dx=dx, dh=dh, dl=dl), device_id_type=MESH).start()

    me = (s, t)
    aux_w = a_aux.at[0, :, pl.ds(0, 4), pl.ds(1, 2)]
    pltpu.make_async_copy(a_aux.at[0, :, 0, pl.ds(1, 2)], b_aux.at[me_slot], lb.at[0]).wait()
    b_aux31 = b_aux.reshape(32, 8, 2, 1, 128).at[pl.ds(0, 31)]
    b_co31 = b_co.reshape(32, 8, 16, 128).at[pl.ds(0, 31)]
    arrived = pltpu.make_async_remote_copy(b_aux31, b_aux31, sb2, rb2, device_id=me, device_id_type=MESH)
    arrived.wait_recv()
    arrived.wait_send()
    flat_aux = b_aux.reshape(32, 8, 2, 1, 128)
    flat_cs = cs5.reshape(5, 2, 32, 8, 128)
    flat_ms = ms5.reshape(5, 32, 8, 128)

    @pl.loop(0, 32)
    def _(i):
        w1 = flat_aux[i, :, 0, 0, :]
        w2 = flat_aux[i, :, 1, 0, :]
        for l, (w, part, first) in enumerate(((w1, high, True), (w1, low, True), (w1, high, False), (w1, low, False), (w2, high, True))):
            co, si = tables(w, lane, part, first)
            flat_cs[l, 0, i] = co
            flat_cs[l, 1, i] = si
            flat_ms[l, i] = kind_rows(w2, 3 + l)

    pltpu.make_async_copy(b_send.at[0, 0], b_co.at[me_slot], lb.at[1]).wait()
    got = pltpu.make_async_remote_copy(b_co31, b_co31, sb, rb, device_id=me, device_id_type=MESH)
    got.wait_recv()
    got.wait_send()

    ev_w = ev[...]
    for l, dim in enumerate((2, 4, 1, 3, 0)):
        rest = [d for d in range(5) if d != dim]
        la, lb_ = (rest[0], rest[1])
        w = wts[3 + l]

        @pl.loop(0, 4)
        def _(i):
            def index(bit):
                at = [slice(None)] * 5
                at[la], at[lb_], at[dim] = i // 2, i % 2, bit
                return tuple(at)

            def grab(ref, lead, bit):
                v = ref[lead + index(bit)]
                return v.reshape((4,) + v.shape[2:])

            x0, x1 = grab(b_co, (), 0), grab(b_co, (), 1)
            m0, m1 = grab(ms5, (l,), 0), grab(ms5, (l,), 1)
            r0 = (grab(cs5, (l, 0), 0), grab(cs5, (l, 1), 0))
            r1 = (grab(cs5, (l, 0), 1), grab(cs5, (l, 1), 1))
            o0, o1 = level(x0, x1, m0, m1, w, r0, r1)
            b_co[index(0)] = o0.astype(jnp.bfloat16).reshape(2, 2, 8, 16, 128)
            b_co[index(1)] = o1.astype(jnp.bfloat16).reshape(2, 2, 8, 16, 128)

    for cc in range(2):
        acc = jnp.zeros((128, 128), jnp.float32)
        for zz in range(4):
            for yy in range(4):
                v = b_co[:, :, :, zz // 2, zz % 2, yy * 2 + cc].reshape(128, 128)
                acc = acc + jnp.dot(v, ev_w, preferred_element_type=jnp.float32)
        osend[:, cc] = acc.astype(jnp.bfloat16).reshape(8, 16, 128)
    sends = []
    for dx, dh, dc in out_peers:
        tx = xs[dx] * 2 + zhs[dh]
        cp = pltpu.make_async_remote_copy(osend.at[tx, cs[dc]], out.at[t], so, ro, device_id=dev(dx=dx, dh=dh, dc=dc), device_id_type=MESH)
        cp.start()
    own = pltpu.make_async_copy(osend.at[x * 2 + zh, c], out.at[t], lb.at[2])
    own.start()
    own.wait()
    o15 = out.at[pl.ds(0, 15)]
    fin = pltpu.make_async_remote_copy(o15, o15, so, ro, device_id=me, device_id_type=MESH)
    fin.wait_send()
    fin.wait_recv()
    fa = pltpu.make_async_remote_copy(a_aux.at[pl.ds(0, 7)], a_aux.at[pl.ds(0, 7)], sa.at[0], ra2.at[0], device_id=me, device_id_type=MESH)
    fa.wait_send()
    fb = pltpu.make_async_remote_copy(a_co.at[pl.ds(0, 7)], a_co.at[pl.ds(0, 7)], sa.at[1], ra.at[0], device_id=me, device_id_type=MESH)
    fb.wait_send()


def per_device(coefficients, phases, classes, blocks, evaluation):
    coef = coefficients.reshape(4, 4, 4, 2, 2, 16, 128)
    wts = blocks.reshape(8, 512, 256)
    vmem = pl.BlockSpec(memory_space=pltpu.VMEM)
    anym = pl.BlockSpec(memory_space=pl.ANY)
    bf, f32, i32 = jnp.bfloat16, jnp.float32, jnp.int32
    dma = pltpu.SemaphoreType.DMA
    result = pl.pallas_call(
        kernel,
        out_shape=jax.ShapeDtypeStruct((16, 16, 128), bf),
        in_specs=[anym, vmem, vmem, anym, vmem],
        out_specs=vmem,
        scratch_shapes=[
            pltpu.VMEM((8, 512, 256), bf),
            pltpu.VMEM((256, 3, 1, 128), i32),
            pltpu.VMEM((8, 8, 4, 16, 128), bf),
            pltpu.VMEM((8, 8, 4, 3, 1, 128), i32),
            pltpu.VMEM((8, 4, 8, 16, 128), bf),
            pltpu.VMEM((2, 2, 2, 2, 2, 8, 16, 128), bf),
            pltpu.VMEM((2, 2, 2, 2, 2, 8, 2, 1, 128), i32),
            pltpu.VMEM((3, 2, 4, 8, 128), f32),
            pltpu.VMEM((3, 4, 8, 128), f32),
            pltpu.VMEM((5, 2, 2, 2, 2, 2, 2, 8, 128), f32),
            pltpu.VMEM((5, 2, 2, 2, 2, 2, 8, 128), f32),
            pltpu.VMEM((8, 2, 16, 128), bf),
            dma, dma((16,)), dma((2,)), dma((8,)), dma((8,)),
            dma, dma, dma, dma, dma, dma, dma((3,)),
        ],
        compiler_params=pltpu.CompilerParams(
            collective_id=0, has_side_effects=True, vmem_limit_bytes=48 * 1024 * 1024),
    )(coef, phases, classes, wts, evaluation)
    return result[None]


def solution(mesh):
    placed = (
        P(("src", "tgt"), None, None),
        P(None, ("src", "tgt"), None),
        P(None, ("src", "tgt")),
        P(),
        P(),
    )
    return jax.shard_map(
        per_device, mesh=mesh, in_specs=placed,
        out_specs=P("tgt", "src", None, None), check_vma=False,
    )
```

time: 387 us -> 72.4 us (0.19)
  the two profiles are of different devices: /device:TPU:4 before, /device:TPU:1 now
where the time goes in v1:
time: 72.4 us; the launch traced here: 72.2 us
  Pallas kernels  67 us (93%)
  local copies, waits for them, and re-layouts  5.13 us (7%)
    pallas_call x1, Pallas kernels, per_device(): pl.pallas_call(kernel, out_shape=jax.ShapeDtypeStruct((16, 16, 128), bf),...  67 us
    unnamed x10, local copies, waits for them, and re-layouts  5.13 us

profile of v1, /device:TPU:1, one launch (start us, length us, event | category | flops | bytes accessed | tf_op | source)
XLA Modules:
  0.0 72.2 jit_solution(11032212032683396057)
XLA Ops:
  0.0 0.0 copy-start.1
  0.0 1.5 %copy.6.ph = f32[8,256,64]{2,1,0:T(8,128)S(1)} copy(f32[8,256,64]{1,2,0:T(8,128)} %param.6) | data formatting | bytes 1048576 | tf_op args[1]
  1.5 0.0 copy-done.1
  1.5 0.0 copy-start
  1.5 1.6 %copy-done = bf16[8,2,2,128,256]{4,3,2,1,0:T(8,128)(2,1)S(1)} copy-done((bf16[8,2,2,128,256]{4,3,2,1,0:T(8,128)(2,1)S(1)}, bf16[8,2,2,128,256]{4,3,2,1,0:T(8,128)(2,1)}, u32[]{:S(2)}) %copy-start) | copy-done | bytes 2097176
  3.1 0.0 copy-start.2
  3.1 0.8 %copy-done.2 = bf16[128,128]{1,0:T(8,128)(2,1)S(1)} copy-done((bf16[128,128]{1,0:T(8,128)(2,1)S(1)}, bf16[128,128]{1,0:T(8,128)(2,1)}, u32[]{:S(2)}) %copy-start.2) | copy-done | bytes 32792
  3.8 0.0 copy-start.3
  3.8 0.7 copy-done.3
  4.5 67.0 %shard_map.55 = bf16[16,16,128]{2,1,0:T(8,128)(2,1)S(1)} custom-call(bf16[4,4,4,2,2,16,128]{6,5,4,3,2,1,0:T(8,128)(2,1)S(1)} %bitcast.4, f32[8,256,64]{2,1,0:T(8,128)S(1)} %copy.6.ph, s32[8,256]{1,0:T(8,128)S(1)} %copy-done.3, bf16[8,512,256]{2,1,0:T(8,128)(2,1)S(1)} %bitcast.3, bf16[128,128]{1,0:T(8,128)(2,1)S(1)} %copy-done.2), custom_call_target="tpu_custom_call" | custom-call | tf_op jit(solution)/shard_map/pallas_call | solution.py:294
  71.5 0.6 copy.8
Async XLA Ops:
  0.0 1.5 %copy-start.1 = (bf16[256,16,128]{2,1,0:T(8,128)(2,1)S(1)}, bf16[256,16,128]{2,1,0:T(8,128)(2,1)}, u32[]{:S(2)}) copy-start(bf16[256,16,128]{2,1,0:T(8,128)(2,1)} %param.5) | copy-start | bytes 3145732
  1.5 1.6 %copy-start = (bf16[8,2,2,128,256]{4,3,2,1,0:T(8,128)(2,1)S(1)}, bf16[8,2,2,128,256]{4,3,2,1,0:T(8,128)(2,1)}, u32[]{:S(2)}) copy-start(bf16[8,2,2,128,256]{4,3,2,1,0:T(8,128)(2,1)} %param.8) | copy-start | bytes 6291460
  3.1 0.8 %copy-start.2 = (bf16[128,128]{1,0:T(8,128)(2,1)S(1)}, bf16[128,128]{1,0:T(8,128)(2,1)}, u32[]{:S(2)}) copy-start(bf16[128,128]{1,0:T(8,128)(2,1)} %ev.1) | copy-start | bytes 98308
  3.8 0.7 copy-start.3

commit v2 on v0

v2 whole, which is shorter than its diff:
```python
import jax
import jax.numpy as jnp
from jax import lax
from jax.experimental import pallas as pl
from jax.experimental.pallas import tpu as pltpu
from jax.sharding import PartitionSpec as P

MESH = pl.DeviceIdType.MESH
SIN = (3.1415927410125732, -5.167712688446045, 2.5501604080200195, -0.5992423295974731,
       0.08208189159631729, -0.007275315932929516, 0.0003952804545406252)
COS = (1.0, -4.93480110168457, 4.058694839477539, -1.3351584672927856,
       0.23502980172634125, -0.025358984246850014, 0.0015939107397571206)
STEP = 10430.378350470453


def horner(coefs, v):
    acc = jnp.full_like(v, coefs[-1])
    for a in coefs[-2::-1]:
        acc = acc * v + a
    return acc


def sin_cos(k):
    u = k.astype(jnp.float32) * (1.0 / 32768.0)
    v = u * u
    return u * horner(SIN, v), horner(COS, v)


def high(w):
    return w >> 16


def low(w):
    return (w << 16) >> 16


def word(a, b):
    return (a << 16) | (b & 0xFFFF)


def tables(k, left, second=True):
    sine, cosine = sin_cos(k)
    sine_r, cosine_r = pltpu.roll(sine, 64, 1), pltpu.roll(cosine, 64, 1)
    out = [(jnp.where(left, cosine, cosine_r), jnp.where(left, -sine, sine_r))]
    if second:
        out.append((jnp.where(left, cosine_r, cosine), jnp.where(left, -sine_r, sine)))
    return out


def expand(rows):
    return jnp.broadcast_to(rows[..., None, :], rows.shape[:-1] + (16, 128))


def butterfly(x0, x1, m0, m1, weights, rot0, rot1):
    g, h = x0.shape[:2]
    shape, rows = (g, h, 16, 128), g * h * 16

    def split(x, m):
        one = x * expand(m).astype(jnp.bfloat16)
        return (x - one).reshape(rows, 128), one.reshape(rows, 128)

    a0, a1 = split(x0, m0)
    b0, b1 = split(x1, m1)
    s = jnp.dot(jnp.concatenate([a0, b0, a1, b1], axis=1), weights, preferred_element_type=jnp.float32)
    outs = []
    for half, (c, sn) in enumerate((rot0, rot1)):
        v = s[:, half * 128:(half + 1) * 128]
        outs.append((v.reshape(shape) * expand(c) + pltpu.roll(v, 64, 1).reshape(shape) * expand(sn)))
    return outs


def kernel(coef, ph_hbm, cls_hbm, wts_hbm, ev_hbm, out,
           ph, cls, ev, wts, aux, a_co, a_aux, b_send, b_co, b_aux, cs3, ms3, cs5, ms5, osend,
           wsem, loc, sa, ra, ra2, sb, rb, sb2, rb2, so, ro, lb, known):
    copies = [pltpu.make_async_copy(a, b, wsem.at[i]) for i, (a, b) in enumerate(
        ((ph_hbm, ph), (cls_hbm, cls), (wts_hbm, wts), (ev_hbm, ev)))]
    for cp in copies:
        cp.start()
    s = lax.axis_index("src")
    t = lax.axis_index("tgt")
    y, zl = s % 4, s // 4
    c, zh, x = t % 2, (t // 2) % 2, t // 4
    x1, x0 = x // 2, x % 2
    ys = [(y + d) % 4 for d in range(4)]
    xs = [x, x1 * 2 + 1 - x0, (1 - x1) * 2 + x0, 3 - x]
    zls = [(zl + d) % 4 for d in range(4)]
    cs = [c, 1 - c]
    zhs = [zh, 1 - zh]
    me = (s, t)

    def dev(dx=0, dy=0, dl=0, dh=0, dc=0):
        return zls[dl] * 4 + ys[dy], xs[dx] * 4 + zhs[dh] * 2 + cs[dc]

    yc_peers = [(dy, dc) for dy in (2, 1, 3, 0) for dc in (0, 1) if (dy, dc) != (0, 0)]
    z_peers = [(dh, dl) for dh in (1, 0) for dl in (0, 2, 1, 3) if (dh, dl) != (0, 0)]
    x_peers = (2, 1, 3)

    barrier = pltpu.get_barrier_semaphore()
    for dh, dl in z_peers:
        pl.semaphore_signal(barrier, inc=1, device_id=dev(dh=dh, dl=dl), device_id_type=MESH)
    for dx in x_peers:
        pl.semaphore_signal(barrier, inc=1, device_id=dev(dx=dx), device_id_type=MESH)
    for dy, dc in yc_peers:
        pl.semaphore_signal(barrier, inc=1, device_id=dev(dy=dy, dc=dc), device_id_type=MESH)

    copies[0].wait()
    copies[1].wait()
    kinds = jnp.concatenate([cls[...], jnp.zeros((56, 256), jnp.int32)], axis=0)

    def fixed(l):
        return jnp.round(ph[l] * STEP).astype(jnp.int32)

    q = [fixed(l) for l in range(8)]
    aux[:, 0, 0, :] = jnp.concatenate([word(q[0], q[1]), word(q[2], kinds)], axis=0).T
    aux[:, 1, 0, :] = jnp.concatenate([word(q[3], q[4]), word(q[5], q[6])], axis=0).T
    aux[:, 2, 0, :] = jnp.concatenate([word(q[7], kinds), jnp.zeros((64, 256), jnp.int32)], axis=0).T
    aux_n = aux.reshape(4, 4, 4, 2, 2, 3, 1, 128)

    pl.semaphore_wait(barrier, 17)
    for dx in x_peers:
        pl.semaphore_signal(known, inc=1, device_id=dev(dx=dx), device_id_type=MESH)

    me_yc = y * 2 + c
    chunks = [(dx, dh) for dx in (2, 3, 1, 0) for dh in (1, 0)]
    for dy, dc in yc_peers:
        pltpu.make_async_remote_copy(
            aux_n.at[:, ys[dy], :, :, cs[dc]], a_aux.at[me_yc], sa.at[0], ra2,
            device_id=dev(dy=dy, dc=dc), device_id_type=MESH).start()
    own_aux = pltpu.make_async_copy(aux_n.at[:, y, :, :, c], a_aux.at[me_yc], lb.at[0])
    own_aux.start()
    own_co = []
    for k, (dx, dh) in enumerate(chunks):
        for dy, dc in yc_peers:
            pltpu.make_async_remote_copy(
                coef.at[:, ys[dy], xs[dx], zhs[dh], cs[dc]], a_co.at[k, me_yc], sa.at[1], ra.at[k],
                device_id=dev(dy=dy, dc=dc), device_id_type=MESH).start()
        own_co.append(pltpu.make_async_copy(coef.at[:, y, xs[dx], zhs[dh], c], a_co.at[k, me_yc], loc.at[k]))
        own_co[-1].start()
    copies[2].wait()
    copies[3].wait()

    def recv(ref, sem, send=False):
        cp = pltpu.make_async_remote_copy(ref, ref, sem, sem, device_id=me, device_id_type=MESH)
        if send:
            cp.wait_send()
        else:
            cp.wait_recv()

    me_slot = (x1, x0, zh, zl // 2, zl % 2)

    def pass_on(k, chunk, src_of, dst, ssem, rsem):
        dx, dh = chunk
        for dl in (2, 1, 3, 0):
            if (dx, dh, dl) == (0, 0, 0):
                pltpu.make_async_copy(src_of(zls[dl]), dst.at[me_slot], rsem.at[k]).start()
            else:
                pltpu.make_async_remote_copy(
                    src_of(zls[dl]), dst.at[me_slot], ssem, rsem.at[k],
                    device_id=dev(dx=dx, dh=dh, dl=dl), device_id_type=MESH).start()

    own_aux.wait()
    recv(a_aux.at[pl.ds(0, 7)], ra2)
    pl.semaphore_wait(known, 3)
    for k, (dx, dh) in enumerate(chunks):
        pass_on(k, (dx, dh), lambda z: a_aux.at[:, z, xs[dx], zhs[dh], pl.ds(1, 2)], b_aux, sb2, rb2)

    left = lax.broadcasted_iota(jnp.int32, (8, 128), 1) < 64

    def kind_rows(words, at):
        return jnp.broadcast_to(low(words)[:, at:at + 1], (8, 128)).astype(jnp.float32)

    for k, (dx, dh) in enumerate(chunks):
        for n in range(4):
            w = a_aux[:, n, xs[dx], zhs[dh], 0, 0, :]
            first, third = tables(high(w), left)
            second, = tables(low(w), left, False)
            for l, (co, si) in enumerate((first, second, third)):
                cs3[l, 0, n] = co
                cs3[l, 1, n] = si
                ms3[l, n] = kind_rows(w, 64 + l)
        own_co[k].wait()
        recv(a_co.at[k, pl.ds(0, 7)], ra.at[k])
        cur = [a_co[k, b] for b in range(8)]
        for l, bit in enumerate((1, 0, 2)):
            lows = [b for b in range(8) if not b & (1 << bit)]
            highs = [b + (1 << bit) for b in lows]

            def rows(table, chosen):
                return jnp.stack([table[:, b] for b in chosen], axis=0)

            def boxes(chosen):
                return jnp.stack([cur[b] for b in chosen], axis=0)

            co, si, mm = cs3[l, 0], cs3[l, 1], ms3[l]
            o0, o1 = butterfly(boxes(lows), boxes(highs), rows(mm, lows), rows(mm, highs), wts[l],
                               (rows(co, lows), rows(si, lows)), (rows(co, highs), rows(si, highs)))
            o0, o1 = o0.astype(jnp.bfloat16), o1.astype(jnp.bfloat16)
            for j in range(4):
                cur[lows[j]], cur[highs[j]] = o0[j], o1[j]
        for b in range(8):
            b_send[k, :, b] = cur[b]
        pass_on(k, (dx, dh), lambda z: b_send.at[k, z], b_co, sb, rb)

    def step(l, dim, fixed_at):
        def grab(ref, lead, bit):
            at = [slice(None)] * 5
            at[dim] = bit
            for d, v in fixed_at.items():
                at[d] = v
            v = ref[tuple(lead) + tuple(at)]
            return v.reshape((4,) + v.shape[2:])

        rots = [tuple(grab(cs5, (l - 3, i), bit) for i in range(2)) for bit in range(2)]
        return butterfly(grab(b_co, (), 0), grab(b_co, (), 1), grab(ms5, (l - 3,), 0), grab(ms5, (l - 3,), 1), wts[l], *rots)

    def step_in_place(l, dim, fixed_at):
        for bit, o in enumerate(step(l, dim, fixed_at)):
            at = [slice(None)] * 5
            at[dim] = bit
            for d, v in fixed_at.items():
                at[d] = v
            b_co[tuple(at)] = o.astype(jnp.bfloat16).reshape(2, 2, 8, 16, 128)

    @pl.loop(0, 4)
    def _(i):
        gx1 = (x1 + 1 + i // 2) % 2
        gx0 = (x0 + i // 2 + i % 2) % 2
        for h in range(2):
            recv(b_aux.at[gx1, gx0, zhs[1 - h]], rb2.at[i * 2 + h])

        @pl.loop(0, 8)
        def _(j):
            at = (gx1, gx0, j // 4, (j // 2) % 2, j % 2)
            w1 = b_aux[at + (slice(None), 0, 0)]
            w2 = b_aux[at + (slice(None), 1, 0)]
            l3, l5 = tables(high(w1), left)
            l4, l6 = tables(low(w1), left)
            l7, = tables(high(w2), left, False)
            for l, (co, si) in enumerate((l3, l4, l5, l6, l7)):
                cs5[(l, 0) + at] = co
                cs5[(l, 1) + at] = si
                ms5[(l,) + at] = kind_rows(w2, 3 + l)

        for h in range(2):
            recv(b_co.at[gx1, gx0, zhs[1 - h]], rb.at[i * 2 + h])
        step_in_place(3, 2, {0: gx1, 1: gx0})
        step_in_place(4, 4, {0: gx1, 1: gx0})

        @pl.when(i % 2 == 1)
        def _():
            for b in range(2):
                step_in_place(5, 1, {0: gx1, 2: b})
            for b in range(2):
                step_in_place(6, 3, {0: gx1, 1: b})

    ev_w = ev[...]
    for dh in (1, 0):
        for dx0 in (1, 0):
            qx0 = (x0 + dx0) % 2
            sums = []
            for o in step(7, 0, {1: qx0, 2: zhs[dh]}):
                sums.append(o.reshape(16, 2, 16, 128).sum(axis=0).reshape(32, 128))
            total = jnp.concatenate(sums, axis=0)
            big = total.astype(jnp.bfloat16)
            small = (total - big.astype(jnp.float32)).astype(jnp.bfloat16)
            r = (jnp.dot(big, ev_w, preferred_element_type=jnp.float32)
                 + jnp.dot(small, ev_w, preferred_element_type=jnp.float32)).astype(jnp.bfloat16)
            osend[:, qx0, zhs[dh]] = r.reshape(2, 2, 16, 128)
            for dx1 in (1, 0):
                for dc in (0, 1):
                    src = osend.at[(x1 + dx1) % 2, qx0, zhs[dh], cs[dc]]
                    if (dx1, dx0, dh, dc) == (0, 0, 0, 0):
                        pltpu.make_async_copy(src, out.at[t], ro).start()
                    else:
                        pltpu.make_async_remote_copy(
                            src, out.at[t], so, ro, device_id=dev(dx=dx1 * 2 + dx0, dh=dh, dc=dc), device_id_type=MESH).start()
    recv(b_aux.reshape(32, 8, 2, 1, 128).at[pl.ds(0, 31)], sb2, True)
    recv(b_co.reshape(32, 8, 16, 128).at[pl.ds(0, 31)], sb, True)
    recv(a_aux.at[pl.ds(0, 7)], sa.at[0], True)
    recv(a_co.at[pl.ds(0, 7)], sa.at[1], True)
    recv(out.at[pl.ds(0, 15)], so, True)
    recv(out, ro)


def per_device(coefficients, phases, classes, blocks, evaluation):
    coef = coefficients.reshape(4, 4, 4, 2, 2, 16, 128)
    wts = blocks.reshape(8, 512, 256)
    vmem = pl.BlockSpec(memory_space=pltpu.VMEM)
    hbm = pl.BlockSpec(memory_space=pltpu.HBM)
    bf, f32, i32 = jnp.bfloat16, jnp.float32, jnp.int32
    dma = pltpu.SemaphoreType.DMA
    result = pl.pallas_call(
        kernel,
        out_shape=jax.ShapeDtypeStruct((16, 16, 128), bf),
        in_specs=[hbm] * 5,
        out_specs=vmem,
        scratch_shapes=[
            pltpu.VMEM((8, 64, 256), f32),
            pltpu.VMEM((8, 256), i32),
            pltpu.VMEM((128, 128), bf),
            pltpu.VMEM((8, 512, 256), bf),
            pltpu.VMEM((256, 3, 1, 128), i32),
            pltpu.VMEM((8, 8, 4, 16, 128), bf),
            pltpu.VMEM((8, 4, 4, 2, 3, 1, 128), i32),
            pltpu.VMEM((8, 4, 8, 16, 128), bf),
            pltpu.VMEM((2, 2, 2, 2, 2, 8, 16, 128), bf),
            pltpu.VMEM((2, 2, 2, 2, 2, 8, 2, 1, 128), i32),
            pltpu.VMEM((3, 2, 4, 8, 128), f32),
            pltpu.VMEM((3, 4, 8, 128), f32),
            pltpu.VMEM((5, 2, 2, 2, 2, 2, 2, 8, 128), f32),
            pltpu.VMEM((5, 2, 2, 2, 2, 2, 8, 128), f32),
            pltpu.VMEM((2, 2, 2, 2, 16, 128), bf),
            dma((4,)), dma((8,)), dma((2,)), dma((8,)), dma,
            dma, dma((8,)), dma, dma((8,)), dma, dma, dma((1,)),
            pltpu.SemaphoreType.REGULAR,
        ],
        compiler_params=pltpu.CompilerParams(
            collective_id=0, has_side_effects=True, vmem_limit_bytes=67043328),
    )(coef, phases.transpose(0, 2, 1), classes, wts, evaluation)
    return result[None]


def solution(mesh):
    placed = (
        P(("src", "tgt"), None, None),
        P(None, ("src", "tgt"), None),
        P(None, ("src", "tgt")),
        P(),
        P(),
    )
    return jax.shard_map(
        per_device, mesh=mesh, in_specs=placed,
        out_specs=P("tgt", "src", None, None), check_vma=False,
    )
```

time: 387 us -> 59.7 us (0.15)
  the two profiles are of different devices: /device:TPU:4 before, /device:TPU:1 now
where the time goes in v2:
time: 59.7 us; the launch traced here: 59.5 us
  Pallas kernels  58.1 us (97%)
  local copies, waits for them, and re-layouts  1.47 us (2%)
    pallas_call x1, Pallas kernels, per_device(): pl.pallas_call(kernel, out_shape=jax.ShapeDtypeStruct((16, 16, 128), bf),...  58.1 us
    unnamed x1, local copies, waits for them, and re-layouts  1.47 us

profile of v2, /device:TPU:1, one launch (start us, length us, event | category | flops | bytes accessed | tf_op | source)
XLA Modules:
  0.0 59.5 jit_solution(14572207124289982149)
XLA Ops:
  0.0 58.1 %shard_map.55 = bf16[16,16,128]{2,1,0:T(8,128)(2,1)} custom-call(bf16[4,4,4,2,2,16,128]{6,5,4,3,2,1,0:T(8,128)(2,1)} %bitcast.5, f32[8,64,256]{2,1,0:T(8,128)} %bitcast.6, s32[8,256]{1,0:T(8,128)} %cls_hbm.1, bf16[8,512,256]{2,1,0:T(8,128)(2,1)} %bitcast.4, bf16[128,128]{1,0:T(8,128)(2,1)} %ev_hbm.1), custom_call_target="tpu_custom_call" | custom-call | tf_op jit(solution)/shard_map/pallas_call | solution.py:292
  58.1 1.5 %copy.7 = bf16[1,16,16,128]{3,2,1,0:T(8,128)(2,1)} copy(bf16[1,16,16,128]{3,2,1,0:T(8,128)(2,1)} %bitcast.7) | data formatting | bytes 131072

commit v3 on v2

--- a/solution.py
+++ b/solution.py
@@ -70,8 +70,8 @@
 
 
 def kernel(coef, ph_hbm, cls_hbm, wts_hbm, ev_hbm, out,
-           ph, cls, ev, wts, aux, a_co, a_aux, b_send, b_co, b_aux, cs3, ms3, cs5, ms5, osend,
-           wsem, loc, sa, ra, ra2, sb, rb, sb2, rb2, so, ro, lb, known):
+           ph, cls, ev, wts, aux, a_co, a_aux, p_send, b_send, b_co, b_aux, q_co, q_aux, qa, cs3, ms3, cs5, ms5, osend,
+           wsem, loc, sa, ra, ra2, sb, rb, sb2, rb2, so, ro, lb, known, sq, rq, rq2, sqa, rqa):
     copies = [pltpu.make_async_copy(a, b, wsem.at[i]) for i, (a, b) in enumerate(
         ((ph_hbm, ph), (cls_hbm, cls), (wts_hbm, wts), (ev_hbm, ev)))]
     for cp in copies:
@@ -83,21 +83,25 @@
     x1, x0 = x // 2, x % 2
     ys = [(y + d) % 4 for d in range(4)]
     xs = [x, x1 * 2 + 1 - x0, (1 - x1) * 2 + x0, 3 - x]
-    zls = [(zl + d) % 4 for d in range(4)]
+    z = zh * 4 + zl
+    zs = [(z + d) % 8 for d in range(8)]
+    ns = [(z + d + 6) % 8 for d in range(8)]
+    n1s, nhs = [v % 4 // 2 for v in ns], [v // 4 for v in ns]
+    zl0s = [zl % 2, 1 - zl % 2]
     cs = [c, 1 - c]
     zhs = [zh, 1 - zh]
     me = (s, t)
 
-    def dev(dx=0, dy=0, dl=0, dh=0, dc=0):
-        return zls[dl] * 4 + ys[dy], xs[dx] * 4 + zhs[dh] * 2 + cs[dc]
+    def dev(dx=0, dy=0, dz=0, dc=0):
+        return zs[dz] % 4 * 4 + ys[dy], xs[dx] * 4 + zs[dz] // 4 * 2 + cs[dc]
 
     yc_peers = [(dy, dc) for dy in (2, 1, 3, 0) for dc in (0, 1) if (dy, dc) != (0, 0)]
-    z_peers = [(dh, dl) for dh in (1, 0) for dl in (0, 2, 1, 3) if (dh, dl) != (0, 0)]
+    z_peers = (4, 3, 5, 2, 6, 1, 7)
     x_peers = (2, 1, 3)
 
     barrier = pltpu.get_barrier_semaphore()
-    for dh, dl in z_peers:
-        pl.semaphore_signal(barrier, inc=1, device_id=dev(dh=dh, dl=dl), device_id_type=MESH)
+    for dz in z_peers:
+        pl.semaphore_signal(barrier, inc=1, device_id=dev(dz=dz), device_id_type=MESH)
     for dx in x_peers:
         pl.semaphore_signal(barrier, inc=1, device_id=dev(dx=dx), device_id_type=MESH)
     for dy, dc in yc_peers:
@@ -114,28 +118,44 @@
     aux[:, 0, 0, :] = jnp.concatenate([word(q[0], q[1]), word(q[2], kinds)], axis=0).T
     aux[:, 1, 0, :] = jnp.concatenate([word(q[3], q[4]), word(q[5], q[6])], axis=0).T
     aux[:, 2, 0, :] = jnp.concatenate([word(q[7], kinds), jnp.zeros((64, 256), jnp.int32)], axis=0).T
-    aux_n = aux.reshape(4, 4, 4, 2, 2, 3, 1, 128)
+    aux_n = aux.reshape(2, 2, 4, 4, 2, 2, 3, 1, 128)
 
     pl.semaphore_wait(barrier, 17)
     for dx in x_peers:
         pl.semaphore_signal(known, inc=1, device_id=dev(dx=dx), device_id_type=MESH)
 
+    for dz in (3, 5, 1, 7):
+        at = (n1s[dz], zl0s[1], slice(None), x, nhs[dz], slice(None))
+        pltpu.make_async_remote_copy(
+            aux_n.at[at], q_aux.at[zl // 2, zh], sq.at[0], rq2, device_id=dev(dz=dz), device_id_type=MESH).start()
+        pltpu.make_async_remote_copy(
+            coef.at[at], q_co.at[zl // 2, zh], sq.at[1], rq, device_id=dev(dz=dz), device_id_type=MESH).start()
+
     me_yc = y * 2 + c
-    chunks = [(dx, dh) for dx in (2, 3, 1, 0) for dh in (1, 0)]
-    for dy, dc in yc_peers:
-        pltpu.make_async_remote_copy(
-            aux_n.at[:, ys[dy], :, :, cs[dc]], a_aux.at[me_yc], sa.at[0], ra2,
-            device_id=dev(dy=dy, dc=dc), device_id_type=MESH).start()
-    own_aux = pltpu.make_async_copy(aux_n.at[:, y, :, :, c], a_aux.at[me_yc], lb.at[0])
-    own_aux.start()
-    own_co = []
-    for k, (dx, dh) in enumerate(chunks):
+    groups = (2, 3, 1, 0)
+    own_aux, own_co = [], {}
+
+    def part(g):
+        return slice(None) if g < 3 else zl0s[0]
+
+    def parities(g):
+        return (1, 0) if g < 3 else (0,)
+
+    for g, dx in enumerate(groups):
         for dy, dc in yc_peers:
             pltpu.make_async_remote_copy(
-                coef.at[:, ys[dy], xs[dx], zhs[dh], cs[dc]], a_co.at[k, me_yc], sa.at[1], ra.at[k],
+                aux_n.at[:, part(g), ys[dy], xs[dx], :, cs[dc]], a_aux.at[g, me_yc, :, part(g)], sa.at[0], ra2.at[g],
                 device_id=dev(dy=dy, dc=dc), device_id_type=MESH).start()
-        own_co.append(pltpu.make_async_copy(coef.at[:, y, xs[dx], zhs[dh], c], a_co.at[k, me_yc], loc.at[k]))
-        own_co[-1].start()
+        own_aux.append(pltpu.make_async_copy(aux_n.at[:, part(g), y, xs[dx], :, c], a_aux.at[g, me_yc, :, part(g)], lb.at[g]))
+        own_aux[-1].start()
+        for p in parities(g):
+            k = g * 2 + 1 - p
+            for dy, dc in yc_peers:
+                pltpu.make_async_remote_copy(
+                    coef.at[:, zl0s[p], ys[dy], xs[dx], :, cs[dc]], a_co.at[k, me_yc], sa.at[1], ra.at[k],
+                    device_id=dev(dy=dy, dc=dc), device_id_type=MESH).start()
+            own_co[k] = pltpu.make_async_copy(coef.at[:, zl0s[p], y, xs[dx], :, c], a_co.at[k, me_yc], loc.at[k])
+            own_co[k].start()
     copies[2].wait()
     copies[3].wait()
 
@@ -148,39 +168,33 @@
 
     me_slot = (x1, x0, zh, zl // 2, zl % 2)
 
-    def pass_on(k, chunk, src_of, dst, ssem, rsem):
-        dx, dh = chunk
-        for dl in (2, 1, 3, 0):
-            if (dx, dh, dl) == (0, 0, 0):
-                pltpu.make_async_copy(src_of(zls[dl]), dst.at[me_slot], rsem.at[k]).start()
-            else:
-                pltpu.make_async_remote_copy(
-                    src_of(zls[dl]), dst.at[me_slot], ssem, rsem.at[k],
-                    device_id=dev(dx=dx, dh=dh, dl=dl), device_id_type=MESH).start()
-
-    own_aux.wait()
-    recv(a_aux.at[pl.ds(0, 7)], ra2)
+    def pass_on(dx, dz, src, dst, ssem, rsem):
+        if (dx, dz) == (0, 0):
+            pltpu.make_async_copy(src, dst.at[me_slot], rsem).start()
+        else:
+            pltpu.make_async_remote_copy(
+                src, dst.at[me_slot], ssem, rsem, device_id=dev(dx=dx, dz=dz), device_id_type=MESH).start()
+
     pl.semaphore_wait(known, 3)
-    for k, (dx, dh) in enumerate(chunks):
-        pass_on(k, (dx, dh), lambda z: a_aux.at[:, z, xs[dx], zhs[dh], pl.ds(1, 2)], b_aux, sb2, rb2)
-
     left = lax.broadcasted_iota(jnp.int32, (8, 128), 1) < 64
 
     def kind_rows(words, at):
         return jnp.broadcast_to(low(words)[:, at:at + 1], (8, 128)).astype(jnp.float32)
 
-    for k, (dx, dh) in enumerate(chunks):
-        for n in range(4):
-            w = a_aux[:, n, xs[dx], zhs[dh], 0, 0, :]
+    def pack(w, v, ref, at):
+        ref[at + (0,)] = w[:4]
+        ref[at + (1,)] = w[4:]
+        ref[at + (2,)] = jnp.where(left[:4], v[:4], pltpu.roll(v, 64, 1)[4:])
+
+    def early_levels(words, chunk):
+        for n, w in enumerate(words):
             first, third = tables(high(w), left)
             second, = tables(low(w), left, False)
             for l, (co, si) in enumerate((first, second, third)):
                 cs3[l, 0, n] = co
                 cs3[l, 1, n] = si
                 ms3[l, n] = kind_rows(w, 64 + l)
-        own_co[k].wait()
-        recv(a_co.at[k, pl.ds(0, 7)], ra.at[k])
-        cur = [a_co[k, b] for b in range(8)]
+        cur = chunk()
         for l, bit in enumerate((1, 0, 2)):
             lows = [b for b in range(8) if not b & (1 << bit)]
             highs = [b + (1 << bit) for b in lows]
@@ -197,9 +211,52 @@
             o0, o1 = o0.astype(jnp.bfloat16), o1.astype(jnp.bfloat16)
             for j in range(4):
                 cur[lows[j]], cur[highs[j]] = o0[j], o1[j]
+        return cur
+
+    def chunk_of(k, own):
+        def load():
+            own.wait()
+            recv(a_co.at[k, pl.ds(0, 7)], ra.at[k])
+            return [a_co[k, b].reshape(4, 16, 128) for b in range(8)]
+        return load
+
+    for g, dx in enumerate(groups):
+        own_aux[g].wait()
+        recv(a_aux.at[g, pl.ds(0, 7), :, part(g)], ra2.at[g])
+        for i in range(8) if g < 3 else range(4):
+            n1, n0, nh = (i // 4, i // 2 % 2, i % 2) if g < 3 else (i // 2, zl0s[0], i % 2)
+            pack(a_aux[g, :, n1, n0, nh, 1, 0, :], a_aux[g, :, n1, n0, nh, 2, 0, :], p_send, (g, n1, n0, nh))
+        for dz in (4, 3, 5, 2, 6, 1, 7, 0) if g < 3 else (4, 2, 6, 0):
+            pass_on(dx, dz, p_send.at[g, n1s[dz], zl0s[dz % 2], nhs[dz]], b_aux, sb2, rb2.at[g])
+        for p in parities(g):
+            k = g * 2 + 1 - p
+            cur = early_levels([a_aux[g, :, n // 2, zl0s[p], n % 2, 0, 0, :] for n in range(4)], chunk_of(k, own_co[k]))
+            for b in range(8):
+                b_send[k, :, b] = cur[b]
+            for dz in (3, 5, 1, 7) if p else (4, 2, 6, 0):
+                pass_on(dx, dz, b_send.at[k, n1s[dz] * 2 + nhs[dz]], b_co, sb, rb.at[k])
+        if g == 0:
+            recv(q_aux, rq2)
+            recv(q_co, rq)
+            for dy, dc in yc_peers:
+                to = dev(dy=dy, dc=dc)
+                pltpu.make_async_remote_copy(
+                    q_aux.at[:, :, ys[dy], cs[dc]], qa.at[me_yc], sqa, rqa, device_id=to, device_id_type=MESH).start()
+                pltpu.make_async_remote_copy(
+                    q_co.at[:, :, ys[dy], cs[dc]], a_co.at[6, me_yc], sa.at[1], ra.at[6], device_id=to, device_id_type=MESH).start()
+            own_qa = pltpu.make_async_copy(q_aux.at[:, :, y, c], qa.at[me_yc], loc.at[8])
+            own_qa.start()
+            own_q = pltpu.make_async_copy(q_co.at[:, :, y, c], a_co.at[6, me_yc], loc.at[6])
+            own_q.start()
+
+    own_qa.wait()
+    recv(qa.at[pl.ds(0, 7)], rqa)
+    for i in range(4):
+        pack(qa[:, i // 2, i % 2, 1, 0, :], qa[:, i // 2, i % 2, 2, 0, :], b_aux, (x1, x0, i % 2, i // 2, zl0s[1]))
+    cur = early_levels([qa[:, n // 2, n % 2, 0, 0, :] for n in range(4)], chunk_of(6, own_q))
+    for n in range(4):
         for b in range(8):
-            b_send[k, :, b] = cur[b]
-        pass_on(k, (dx, dh), lambda z: b_send.at[k, z], b_co, sb, rb)
+            b_co[x1, x0, n % 2, n // 2, zl0s[1], b] = cur[b][n]
 
     def step(l, dim, fixed_at):
         def grab(ref, lead, bit):
@@ -208,7 +265,7 @@
             for d, v in fixed_at.items():
                 at[d] = v
             v = ref[tuple(lead) + tuple(at)]
-            return v.reshape((4,) + v.shape[2:])
+            return v.reshape((-1,) + v.shape[-3 + (ref is not b_co):])
 
         rots = [tuple(grab(cs5, (l - 3, i), bit) for i in range(2)) for bit in range(2)]
         return butterfly(grab(b_co, (), 0), grab(b_co, (), 1), grab(ms5, (l - 3,), 0), grab(ms5, (l - 3,), 1), wts[l], *rots)
@@ -219,20 +276,26 @@
             at[dim] = bit
             for d, v in fixed_at.items():
                 at[d] = v
-            b_co[tuple(at)] = o.astype(jnp.bfloat16).reshape(2, 2, 8, 16, 128)
+            b_co[tuple(at)] = o.astype(jnp.bfloat16).reshape((2,) * (4 - len(fixed_at)) + (8, 16, 128))
 
     @pl.loop(0, 4)
     def _(i):
         gx1 = (x1 + 1 + i // 2) % 2
         gx0 = (x0 + i // 2 + i % 2) % 2
-        for h in range(2):
-            recv(b_aux.at[gx1, gx0, zhs[1 - h]], rb2.at[i * 2 + h])
+        @pl.when(i < 3)
+        def _():
+            recv(b_aux.at[gx1, gx0], rb2.at[i])
+
+        @pl.when(i == 3)
+        def _():
+            recv(b_aux.at[x1, x0, :, :, zl0s[0]], rb2.at[3])
 
         @pl.loop(0, 8)
         def _(j):
             at = (gx1, gx0, j // 4, (j // 2) % 2, j % 2)
-            w1 = b_aux[at + (slice(None), 0, 0)]
-            w2 = b_aux[at + (slice(None), 1, 0)]
+            w1 = jnp.concatenate([b_aux[at + (0,)], b_aux[at + (1,)]], axis=0)
+            w2 = b_aux[at + (2,)]
+            w2 = jnp.concatenate([w2, pltpu.roll(w2, 64, 1)], axis=0)
             l3, l5 = tables(high(w1), left)
             l4, l6 = tables(low(w1), left)
             l7, = tables(high(w2), left, False)
@@ -242,8 +305,13 @@
                 ms5[(l,) + at] = kind_rows(w2, 3 + l)
 
         for h in range(2):
-            recv(b_co.at[gx1, gx0, zhs[1 - h]], rb.at[i * 2 + h])
-        step_in_place(3, 2, {0: gx1, 1: gx0})
+            if h:
+                recv(b_co.at[gx1, gx0, :, :, zl0s[0]], rb.at[i * 2 + 1])
+            else:
+                @pl.when(i < 3)
+                def _():
+                    recv(b_co.at[gx1, gx0, :, :, zl0s[1]], rb.at[i * 2])
+            step_in_place(3, 2, {0: gx1, 1: gx0, 4: zl0s[1 - h]})
         step_in_place(4, 4, {0: gx1, 1: gx0})
 
         @pl.when(i % 2 == 1)
@@ -254,8 +322,9 @@
                 step_in_place(6, 3, {0: gx1, 1: b})
 
     ev_w = ev[...]
-    for dh in (1, 0):
-        for dx0 in (1, 0):
+    mine = x * 4 + nhs[0] * 2 + c
+    for dx0 in (0, 1):
+        for dh in (1, 0):
             qx0 = (x0 + dx0) % 2
             sums = []
             for o in step(7, 0, {1: qx0, 2: zhs[dh]}):
@@ -269,21 +338,21 @@
             for dx1 in (1, 0):
                 for dc in (0, 1):
                     src = osend.at[(x1 + dx1) % 2, qx0, zhs[dh], cs[dc]]
-                    if (dx1, dx0, dh, dc) == (0, 0, 0, 0):
-                        pltpu.make_async_copy(src, out.at[t], ro).start()
-                    else:
-                        pltpu.make_async_remote_copy(
-                            src, out.at[t], so, ro, device_id=dev(dx=dx1 * 2 + dx0, dh=dh, dc=dc), device_id_type=MESH).start()
-    recv(b_aux.reshape(32, 8, 2, 1, 128).at[pl.ds(0, 31)], sb2, True)
-    recv(b_co.reshape(32, 8, 16, 128).at[pl.ds(0, 31)], sb, True)
-    recv(a_aux.at[pl.ds(0, 7)], sa.at[0], True)
+                    to = (ns[0] % 4 * 4 + y, xs[dx1 * 2 + dx0] * 4 + zhs[dh] * 2 + cs[dc])
+                    pltpu.make_async_remote_copy(src, out.at[mine], so, ro, device_id=to, device_id_type=MESH).start()
+    recv(b_aux.reshape(32, 3, 4, 128).at[pl.ds(0, 27)], sb2, True)
+    recv(b_co.reshape(32, 8, 16, 128).at[pl.ds(0, 27)], sb, True)
+    recv(aux.at[pl.ds(0, 196)], sa.at[0], True)
     recv(a_co.at[pl.ds(0, 7)], sa.at[1], True)
-    recv(out.at[pl.ds(0, 15)], so, True)
+    recv(q_aux, sq.at[0], True)
+    recv(q_co, sq.at[1], True)
+    recv(qa.at[pl.ds(0, 7)], sqa, True)
+    recv(out, so, True)
     recv(out, ro)
 
 
 def per_device(coefficients, phases, classes, blocks, evaluation):
-    coef = coefficients.reshape(4, 4, 4, 2, 2, 16, 128)
+    coef = coefficients.reshape(2, 2, 4, 4, 2, 2, 16, 128)
     wts = blocks.reshape(8, 512, 256)
     vmem = pl.BlockSpec(memory_space=pltpu.VMEM)
     hbm = pl.BlockSpec(memory_space=pltpu.HBM)
@@ -291,7 +360,7 @@
     dma = pltpu.SemaphoreType.DMA
     result = pl.pallas_call(
         kernel,
-        out_shape=jax.ShapeDtypeStruct((16, 16, 128), bf),
+        out_shape=pltpu.VMEM((16, 16, 128), bf),
         in_specs=[hbm] * 5,
         out_specs=vmem,
         scratch_shapes=[
@@ -300,22 +369,26 @@
             pltpu.VMEM((128, 128), bf),
             pltpu.VMEM((8, 512, 256), bf),
             pltpu.VMEM((256, 3, 1, 128), i32),
-            pltpu.VMEM((8, 8, 4, 16, 128), bf),
-            pltpu.VMEM((8, 4, 4, 2, 3, 1, 128), i32),
+            pltpu.VMEM((8, 8, 2, 2, 16, 128), bf),
+            pltpu.VMEM((4, 8, 2, 2, 2, 3, 1, 128), i32),
+            pltpu.VMEM((4, 2, 2, 2, 3, 4, 128), i32),
             pltpu.VMEM((8, 4, 8, 16, 128), bf),
             pltpu.VMEM((2, 2, 2, 2, 2, 8, 16, 128), bf),
-            pltpu.VMEM((2, 2, 2, 2, 2, 8, 2, 1, 128), i32),
+            pltpu.VMEM((2, 2, 2, 2, 2, 3, 4, 128), i32),
+            pltpu.VMEM((2, 2, 4, 2, 16, 128), bf),
+            pltpu.VMEM((2, 2, 4, 2, 3, 1, 128), i32),
+            pltpu.VMEM((8, 2, 2, 3, 1, 128), i32),
             pltpu.VMEM((3, 2, 4, 8, 128), f32),
             pltpu.VMEM((3, 4, 8, 128), f32),
             pltpu.VMEM((5, 2, 2, 2, 2, 2, 2, 8, 128), f32),
             pltpu.VMEM((5, 2, 2, 2, 2, 2, 8, 128), f32),
             pltpu.VMEM((2, 2, 2, 2, 16, 128), bf),
-            dma((4,)), dma((8,)), dma((2,)), dma((8,)), dma,
-            dma, dma((8,)), dma, dma((8,)), dma, dma, dma((1,)),
-            pltpu.SemaphoreType.REGULAR,
+            dma((4,)), dma((9,)), dma((2,)), dma((8,)), dma((4,)),
+            dma, dma((8,)), dma, dma((4,)), dma, dma, dma((4,)),
+            pltpu.SemaphoreType.REGULAR, dma((2,)), dma, dma, dma, dma,
         ],
         compiler_params=pltpu.CompilerParams(
-            collective_id=0, has_side_effects=True, vmem_limit_bytes=67043328),
+            collective_id=0, has_side_effects=True, vmem_limit_bytes=66912256),
     )(coef, phases.transpose(0, 2, 1), classes, wts, evaluation)
     return result[None]
 

time: 59.7 us -> 52.5 us (0.88)
  Pallas kernels: 58.1 us -> 51.8 us
  local copies, waits for them, and re-layouts: 1.47 us -> 0.63 us
    pallas_call x1, Pallas kernels: 58.1 us -> 51.8 us  [per_device(): pl.pallas_call(kernel, out_shape=pltpu.VMEM((16, 16, 128), bf), in_specs=...]
    unnamed x1, local copies, waits for them, and re-layouts: 1.47 us -> 0.63 us
where the time goes in v3:
time: 52.5 us; the launch traced here: 52.4 us
  Pallas kernels  51.8 us (99%)
  local copies, waits for them, and re-layouts  0.63 us (1%)
    pallas_call x1, Pallas kernels, per_device(): pl.pallas_call(kernel, out_shape=pltpu.VMEM((16, 16, 128), bf), in_specs=...  51.8 us

profile of v3, /device:TPU:1, one launch (start us, length us, event | category | flops | bytes accessed | tf_op | source)
XLA Modules:
  0.0 52.4 jit_solution(10257740104094980391)
XLA Ops:
  0.0 51.8 %shard_map.55 = bf16[16,16,128]{2,1,0:T(8,128)(2,1)S(1)} custom-call(bf16[2,2,4,4,2,2,16,128]{7,6,5,4,3,2,1,0:T(8,128)(2,1)} %bitcast.6, f32[8,64,256]{2,1,0:T(8,128)} %bitcast.7, s32[8,256]{1,0:T(8,128)} %cls_hbm.1, bf16[8,512,256]{2,1,0:T(8,128)(2,1)} %bitcast.5, bf16[128,128]{1,0:T(8,128)(2,1)} %ev_hbm.1), custom_call_target="tpu_custom_call" | custom-call | tf_op jit(solution)/shard_map/pallas_call | solution.py:361
  51.8 0.6 %copy.7 = bf16[1,16,16,128]{3,2,1,0:T(8,128)(2,1)} copy(bf16[1,16,16,128]{3,2,1,0:T(8,128)(2,1)S(1)} %bitcast.4) | data formatting | bytes 131072

commit v4 on v3

--- a/solution.py
+++ b/solution.py
@@ -6,10 +6,8 @@
 from jax.sharding import PartitionSpec as P
 
 MESH = pl.DeviceIdType.MESH
-SIN = (3.1415927410125732, -5.167712688446045, 2.5501604080200195, -0.5992423295974731,
-       0.08208189159631729, -0.007275315932929516, 0.0003952804545406252)
-COS = (1.0, -4.93480110168457, 4.058694839477539, -1.3351584672927856,
-       0.23502980172634125, -0.025358984246850014, 0.0015939107397571206)
+SIN = (3.141592502593994, -5.167698860168457, 2.5499982833862305, -0.59855055809021, 0.0807478204369545, -0.00608947454020381)
+COS = (1.0, -4.93480110168457, 4.058694839477539, -1.3351584672927856, 0.23502980172634125, -0.025358984246850014, 0.0015939107397571206)
 STEP = 10430.378350470453
 
 
@@ -70,7 +68,7 @@
 
 
 def kernel(coef, ph_hbm, cls_hbm, wts_hbm, ev_hbm, out,
-           ph, cls, ev, wts, aux, a_co, a_aux, p_send, b_send, b_co, b_aux, q_co, q_aux, qa, cs3, ms3, cs5, ms5, osend,
+           ph, cls, ev, wts, aux, a_co, a_aux, p_send, b_send, b_co, b_aux, q_co, q_aux, qa, cs3, ms3, cs5, ms5, acc, osend,
            wsem, loc, sa, ra, ra2, sb, rb, sb2, rb2, so, ro, lb, known, sq, rq, rq2, sqa, rqa):
     copies = [pltpu.make_async_copy(a, b, wsem.at[i]) for i, (a, b) in enumerate(
         ((ph_hbm, ph), (cls_hbm, cls), (wts_hbm, wts), (ev_hbm, ev)))]
@@ -144,9 +142,9 @@
     for g, dx in enumerate(groups):
         for dy, dc in yc_peers:
             pltpu.make_async_remote_copy(
-                aux_n.at[:, part(g), ys[dy], xs[dx], :, cs[dc]], a_aux.at[g, me_yc, :, part(g)], sa.at[0], ra2.at[g],
+                aux_n.at[:, part(g), ys[dy], xs[dx], :, cs[dc]], a_aux.at[g, :, part(g), :, :, pl.ds(me_yc, 1)], sa.at[0], ra2.at[g],
                 device_id=dev(dy=dy, dc=dc), device_id_type=MESH).start()
-        own_aux.append(pltpu.make_async_copy(aux_n.at[:, part(g), y, xs[dx], :, c], a_aux.at[g, me_yc, :, part(g)], lb.at[g]))
+        own_aux.append(pltpu.make_async_copy(aux_n.at[:, part(g), y, xs[dx], :, c], a_aux.at[g, :, part(g), :, :, pl.ds(me_yc, 1)], lb.at[g]))
         own_aux[-1].start()
         for p in parities(g):
             k = g * 2 + 1 - p
@@ -168,12 +166,12 @@
 
     me_slot = (x1, x0, zh, zl // 2, zl % 2)
 
-    def pass_on(dx, dz, src, dst, ssem, rsem):
+    def pass_on(dx, dz, src, dst, ssem, rsem, half=()):
         if (dx, dz) == (0, 0):
-            pltpu.make_async_copy(src, dst.at[me_slot], rsem).start()
+            pltpu.make_async_copy(src, dst.at[me_slot + half], rsem).start()
         else:
             pltpu.make_async_remote_copy(
-                src, dst.at[me_slot], ssem, rsem, device_id=dev(dx=dx, dz=dz), device_id_type=MESH).start()
+                src, dst.at[me_slot + half], ssem, rsem, device_id=dev(dx=dx, dz=dz), device_id_type=MESH).start()
 
     pl.semaphore_wait(known, 3)
     left = lax.broadcasted_iota(jnp.int32, (8, 128), 1) < 64
@@ -185,6 +183,10 @@
         ref[at + (0,)] = w[:4]
         ref[at + (1,)] = w[4:]
         ref[at + (2,)] = jnp.where(left[:4], v[:4], pltpu.roll(v, 64, 1)[4:])
+
+    def pass_chunk(k, dx, p, hf):
+        for dz in (3, 5, 1, 7) if p else (4, 2, 6, 0):
+            pass_on(dx, dz, b_send.at[k, n1s[dz] * 2 + nhs[dz], pl.ds(hf * 4, 4)], b_co, sb, rb.at[k, hf], (hf,))
 
     def early_levels(words, chunk):
         for n, w in enumerate(words):
@@ -222,77 +224,81 @@
 
     for g, dx in enumerate(groups):
         own_aux[g].wait()
-        recv(a_aux.at[g, pl.ds(0, 7), :, part(g)], ra2.at[g])
+        recv(aux.at[pl.ds(0, 56 if g < 3 else 28)], ra2.at[g])
         for i in range(8) if g < 3 else range(4):
             n1, n0, nh = (i // 4, i // 2 % 2, i % 2) if g < 3 else (i // 2, zl0s[0], i % 2)
-            pack(a_aux[g, :, n1, n0, nh, 1, 0, :], a_aux[g, :, n1, n0, nh, 2, 0, :], p_send, (g, n1, n0, nh))
+            pack(a_aux[g, n1, n0, nh, 1], a_aux[g, n1, n0, nh, 2], p_send, (g, n1, n0, nh))
         for dz in (4, 3, 5, 2, 6, 1, 7, 0) if g < 3 else (4, 2, 6, 0):
             pass_on(dx, dz, p_send.at[g, n1s[dz], zl0s[dz % 2], nhs[dz]], b_aux, sb2, rb2.at[g])
         for p in parities(g):
             k = g * 2 + 1 - p
-            cur = early_levels([a_aux[g, :, n // 2, zl0s[p], n % 2, 0, 0, :] for n in range(4)], chunk_of(k, own_co[k]))
+            cur = early_levels([a_aux[g, n // 2, zl0s[p], n % 2, 0] for n in range(4)], chunk_of(k, own_co[k]))
             for b in range(8):
                 b_send[k, :, b] = cur[b]
-            for dz in (3, 5, 1, 7) if p else (4, 2, 6, 0):
-                pass_on(dx, dz, b_send.at[k, n1s[dz] * 2 + nhs[dz]], b_co, sb, rb.at[k])
+            pass_chunk(k, dx, p, 0)
+            if g < 2:
+                pass_chunk(k, dx, p, 1)
         if g == 0:
             recv(q_aux, rq2)
             recv(q_co, rq)
             for dy, dc in yc_peers:
                 to = dev(dy=dy, dc=dc)
                 pltpu.make_async_remote_copy(
-                    q_aux.at[:, :, ys[dy], cs[dc]], qa.at[me_yc], sqa, rqa, device_id=to, device_id_type=MESH).start()
+                    q_aux.at[:, :, ys[dy], cs[dc]], qa.at[:, :, :, pl.ds(me_yc, 1)], sqa, rqa, device_id=to, device_id_type=MESH).start()
                 pltpu.make_async_remote_copy(
                     q_co.at[:, :, ys[dy], cs[dc]], a_co.at[6, me_yc], sa.at[1], ra.at[6], device_id=to, device_id_type=MESH).start()
-            own_qa = pltpu.make_async_copy(q_aux.at[:, :, y, c], qa.at[me_yc], loc.at[8])
+            own_qa = pltpu.make_async_copy(q_aux.at[:, :, y, c], qa.at[:, :, :, pl.ds(me_yc, 1)], loc.at[8])
             own_qa.start()
             own_q = pltpu.make_async_copy(q_co.at[:, :, y, c], a_co.at[6, me_yc], loc.at[6])
             own_q.start()
 
+    pass_chunk(4, 1, 1, 1)
+    pass_chunk(5, 1, 0, 1)
+    pass_chunk(7, 0, 0, 1)
     own_qa.wait()
-    recv(qa.at[pl.ds(0, 7)], rqa)
+    recv(aux.at[pl.ds(0, 28)], rqa)
     for i in range(4):
-        pack(qa[:, i // 2, i % 2, 1, 0, :], qa[:, i // 2, i % 2, 2, 0, :], b_aux, (x1, x0, i % 2, i // 2, zl0s[1]))
-    cur = early_levels([qa[:, n // 2, n % 2, 0, 0, :] for n in range(4)], chunk_of(6, own_q))
+        pack(qa[i // 2, i % 2, 1], qa[i // 2, i % 2, 2], b_aux, (x1, x0, i % 2, i // 2, zl0s[1]))
+    cur = early_levels([qa[n // 2, n % 2, 0] for n in range(4)], chunk_of(6, own_q))
     for n in range(4):
         for b in range(8):
-            b_co[x1, x0, n % 2, n // 2, zl0s[1], b] = cur[b][n]
-
-    def step(l, dim, fixed_at):
-        def grab(ref, lead, bit):
-            at = [slice(None)] * 5
-            at[dim] = bit
-            for d, v in fixed_at.items():
-                at[d] = v
-            v = ref[tuple(lead) + tuple(at)]
-            return v.reshape((-1,) + v.shape[-3 + (ref is not b_co):])
-
-        rots = [tuple(grab(cs5, (l - 3, i), bit) for i in range(2)) for bit in range(2)]
-        return butterfly(grab(b_co, (), 0), grab(b_co, (), 1), grab(ms5, (l - 3,), 0), grab(ms5, (l - 3,), 1), wts[l], *rots)
-
-    def step_in_place(l, dim, fixed_at):
-        for bit, o in enumerate(step(l, dim, fixed_at)):
-            at = [slice(None)] * 5
-            at[dim] = bit
-            for d, v in fixed_at.items():
-                at[d] = v
-            b_co[tuple(at)] = o.astype(jnp.bfloat16).reshape((2,) * (4 - len(fixed_at)) + (8, 16, 128))
-
-    @pl.loop(0, 4)
-    def _(i):
-        gx1 = (x1 + 1 + i // 2) % 2
-        gx0 = (x0 + i // 2 + i % 2) % 2
-        @pl.when(i < 3)
-        def _():
-            recv(b_aux.at[gx1, gx0], rb2.at[i])
-
-        @pl.when(i == 3)
-        def _():
-            recv(b_aux.at[x1, x0, :, :, zl0s[0]], rb2.at[3])
-
-        @pl.loop(0, 8)
-        def _(j):
-            at = (gx1, gx0, j // 4, (j // 2) % 2, j % 2)
+            b_co[x1, x0, n % 2, n // 2, zl0s[1], b // 4, b % 4] = cur[b][n]
+
+    def place(dim, bit, fixed_at):
+        at = [slice(None)] * 5
+        at[dim] = bit
+        for d, v in fixed_at.items():
+            at[d] = v
+        return tuple(at)
+
+    def step(l, dim, fixed_at, hf):
+        height = 8 if hf is None else 4
+
+        def boxes(bit):
+            at = place(dim, bit, fixed_at)
+            return b_co[at if hf is None else at + (hf,)].reshape(-1, height, 16, 128)
+
+        def rows(ref, lead, bit):
+            at = lead + place(dim, bit, fixed_at)
+            return ref[at if hf is None else at + (pl.ds(hf * 4, 4),)].reshape(-1, height, 128)
+
+        rots = [tuple(rows(cs5, (l - 3, i), bit) for i in range(2)) for bit in range(2)]
+        return butterfly(boxes(0), boxes(1), rows(ms5, (l - 3,), 0), rows(ms5, (l - 3,), 1), wts[l], *rots)
+
+    def step_in_place(l, dim, fixed_at, hf=None):
+        for bit, o in enumerate(step(l, dim, fixed_at, hf)):
+            at = place(dim, bit, fixed_at)
+            lead = (2,) * (4 - len(fixed_at))
+            if hf is None:
+                b_co[at] = o.astype(jnp.bfloat16).reshape(lead + (2, 4, 16, 128))
+            else:
+                b_co[at + (hf,)] = o.astype(jnp.bfloat16).reshape(lead + (4, 16, 128))
+
+    def late_tables(gx1, gx0):
+        @pl.loop(0, 2)
+        def _(z1):
+          for j in range(4):
+            at = (gx1, gx0, j // 2, z1, j % 2)
             w1 = jnp.concatenate([b_aux[at + (0,)], b_aux[at + (1,)]], axis=0)
             w2 = b_aux[at + (2,)]
             w2 = jnp.concatenate([w2, pltpu.roll(w2, 64, 1)], axis=0)
@@ -304,49 +310,68 @@
                 cs5[(l, 1) + at] = si
                 ms5[(l,) + at] = kind_rows(w2, 3 + l)
 
+    far = 1 - x1
+
+    @pl.loop(0, 2)
+    def _(i):
+        gx0 = (x0 + i) % 2
+        recv(b_aux.at[far, gx0], rb2.at[i])
+        late_tables(far, gx0)
         for h in range(2):
-            if h:
-                recv(b_co.at[gx1, gx0, :, :, zl0s[0]], rb.at[i * 2 + 1])
-            else:
-                @pl.when(i < 3)
-                def _():
-                    recv(b_co.at[gx1, gx0, :, :, zl0s[1]], rb.at[i * 2])
-            step_in_place(3, 2, {0: gx1, 1: gx0, 4: zl0s[1 - h]})
-        step_in_place(4, 4, {0: gx1, 1: gx0})
-
-        @pl.when(i % 2 == 1)
-        def _():
-            for b in range(2):
-                step_in_place(5, 1, {0: gx1, 2: b})
-            for b in range(2):
-                step_in_place(6, 3, {0: gx1, 1: b})
-
+            for hf in range(2):
+                recv(b_co.at[far, gx0, :, :, zl0s[1 - h], hf], rb.at[i * 2 + h, hf])
+            step_in_place(3, 2, {0: far, 1: gx0, 4: zl0s[1 - h]})
+        step_in_place(4, 4, {0: far, 1: gx0})
+
+    for b in range(2):
+        step_in_place(5, 1, {0: far, 2: b})
+    for b in range(2):
+        step_in_place(6, 3, {0: far, 1: b})
+
+    near = 1 - x0
+    recv(b_aux.at[x1, near], rb2.at[2])
+    late_tables(x1, near)
+    recv(b_aux.at[x1, x0, :, :, zl0s[0]], rb2.at[3])
+    late_tables(x1, x0)
+    step_in_place(3, 2, {0: x1, 1: x0, 4: zl0s[1]})
     ev_w = ev[...]
     mine = x * 4 + nhs[0] * 2 + c
-    for dx0 in (0, 1):
-        for dh in (1, 0):
-            qx0 = (x0 + dx0) % 2
-            sums = []
-            for o in step(7, 0, {1: qx0, 2: zhs[dh]}):
-                sums.append(o.reshape(16, 2, 16, 128).sum(axis=0).reshape(32, 128))
-            total = jnp.concatenate(sums, axis=0)
-            big = total.astype(jnp.bfloat16)
-            small = (total - big.astype(jnp.float32)).astype(jnp.bfloat16)
-            r = (jnp.dot(big, ev_w, preferred_element_type=jnp.float32)
-                 + jnp.dot(small, ev_w, preferred_element_type=jnp.float32)).astype(jnp.bfloat16)
-            osend[:, qx0, zhs[dh]] = r.reshape(2, 2, 16, 128)
-            for dx1 in (1, 0):
+    for hf in range(2):
+        for h in range(2):
+            recv(b_co.at[x1, near, :, :, zl0s[1 - h], hf], rb.at[4 + h, hf])
+            step_in_place(3, 2, {0: x1, 1: near, 4: zl0s[1 - h]}, hf)
+        step_in_place(4, 4, {0: x1, 1: near}, hf)
+        recv(b_co.at[x1, x0, :, :, zl0s[0], hf], rb.at[7, hf])
+        step_in_place(3, 2, {0: x1, 1: x0, 4: zl0s[0]}, hf)
+        step_in_place(4, 4, {0: x1, 1: x0}, hf)
+        step_in_place(5, 1, {0: x1}, hf)
+        step_in_place(6, 3, {0: x1}, hf)
+        sums = [[o.reshape(2, 4, 2, 2, 16, 128).sum(axis=(1, 2)) for o in step(7, 0, {1: q}, hf)] for q in range(2)]
+        if hf == 0:
+            for q in range(2):
+                for bit in range(2):
+                    acc[bit, q] = sums[q][bit]
+            continue
+        total = jnp.concatenate([(sums[q][bit] + acc[bit, q]).reshape(64, 128) for bit in range(2) for q in range(2)], axis=0)
+        big = total.astype(jnp.bfloat16)
+        small = (total - big.astype(jnp.float32)).astype(jnp.bfloat16)
+        r = (jnp.dot(big, ev_w, preferred_element_type=jnp.float32)
+             + jnp.dot(small, ev_w, preferred_element_type=jnp.float32)).astype(jnp.bfloat16)
+        osend[...] = r.reshape(2, 2, 2, 2, 16, 128)
+        for dx in (2, 3, 1, 0):
+            for dh in (1, 0):
                 for dc in (0, 1):
-                    src = osend.at[(x1 + dx1) % 2, qx0, zhs[dh], cs[dc]]
-                    to = (ns[0] % 4 * 4 + y, xs[dx1 * 2 + dx0] * 4 + zhs[dh] * 2 + cs[dc])
-                    pltpu.make_async_remote_copy(src, out.at[mine], so, ro, device_id=to, device_id_type=MESH).start()
+                    to = (ns[0] % 4 * 4 + y, xs[dx] * 4 + zhs[dh] * 2 + cs[dc])
+                    pltpu.make_async_remote_copy(
+                        osend.at[xs[dx] // 2, xs[dx] % 2, zhs[dh], cs[dc]], out.at[mine], so, ro,
+                        device_id=to, device_id_type=MESH).start()
     recv(b_aux.reshape(32, 3, 4, 128).at[pl.ds(0, 27)], sb2, True)
     recv(b_co.reshape(32, 8, 16, 128).at[pl.ds(0, 27)], sb, True)
     recv(aux.at[pl.ds(0, 196)], sa.at[0], True)
     recv(a_co.at[pl.ds(0, 7)], sa.at[1], True)
     recv(q_aux, sq.at[0], True)
     recv(q_co, sq.at[1], True)
-    recv(qa.at[pl.ds(0, 7)], sqa, True)
+    recv(aux.at[pl.ds(0, 28)], sqa, True)
     recv(out, so, True)
     recv(out, ro)
 
@@ -370,21 +395,22 @@
             pltpu.VMEM((8, 512, 256), bf),
             pltpu.VMEM((256, 3, 1, 128), i32),
             pltpu.VMEM((8, 8, 2, 2, 16, 128), bf),
-            pltpu.VMEM((4, 8, 2, 2, 2, 3, 1, 128), i32),
+            pltpu.VMEM((4, 2, 2, 2, 3, 8, 128), i32),
             pltpu.VMEM((4, 2, 2, 2, 3, 4, 128), i32),
             pltpu.VMEM((8, 4, 8, 16, 128), bf),
-            pltpu.VMEM((2, 2, 2, 2, 2, 8, 16, 128), bf),
+            pltpu.VMEM((2, 2, 2, 2, 2, 2, 4, 16, 128), bf),
             pltpu.VMEM((2, 2, 2, 2, 2, 3, 4, 128), i32),
             pltpu.VMEM((2, 2, 4, 2, 16, 128), bf),
             pltpu.VMEM((2, 2, 4, 2, 3, 1, 128), i32),
-            pltpu.VMEM((8, 2, 2, 3, 1, 128), i32),
+            pltpu.VMEM((2, 2, 3, 8, 128), i32),
             pltpu.VMEM((3, 2, 4, 8, 128), f32),
             pltpu.VMEM((3, 4, 8, 128), f32),
             pltpu.VMEM((5, 2, 2, 2, 2, 2, 2, 8, 128), f32),
             pltpu.VMEM((5, 2, 2, 2, 2, 2, 8, 128), f32),
+            pltpu.VMEM((2, 2, 2, 2, 16, 128), f32),
             pltpu.VMEM((2, 2, 2, 2, 16, 128), bf),
             dma((4,)), dma((9,)), dma((2,)), dma((8,)), dma((4,)),
-            dma, dma((8,)), dma, dma((4,)), dma, dma, dma((4,)),
+            dma, dma((8, 2)), dma, dma((4,)), dma, dma, dma((4,)),
             pltpu.SemaphoreType.REGULAR, dma((2,)), dma, dma, dma, dma,
         ],
         compiler_params=pltpu.CompilerParams(

time: 52.5 us -> 51.2 us (0.975)
  Pallas kernels: 51.8 us -> 50.5 us
    pallas_call x1, Pallas kernels: 51.8 us -> 50.5 us  [per_device(): pl.pallas_call(kernel, out_shape=pltpu.VMEM((16, 16, 128), bf), in_specs=...]
where the time goes in v4:
time: 51.2 us; the launch traced here: 51.1 us
  Pallas kernels  50.5 us (99%)
  local copies, waits for them, and re-layouts  0.63 us (1%)
    pallas_call x1, Pallas kernels, per_device(): pl.pallas_call(kernel, out_shape=pltpu.VMEM((16, 16, 128), bf), in_specs=...  50.5 us

profile of v4, /device:TPU:1, one launch (start us, length us, event | category | flops | bytes accessed | tf_op | source)
XLA Modules:
  0.0 51.1 jit_solution(10634808669036660413)
XLA Ops:
  0.0 50.5 %shard_map.55 = bf16[16,16,128]{2,1,0:T(8,128)(2,1)S(1)} custom-call(bf16[2,2,4,4,2,2,16,128]{7,6,5,4,3,2,1,0:T(8,128)(2,1)} %bitcast.6, f32[8,64,256]{2,1,0:T(8,128)} %bitcast.7, s32[8,256]{1,0:T(8,128)} %cls_hbm.1, bf16[8,512,256]{2,1,0:T(8,128)(2,1)} %bitcast.5, bf16[128,128]{1,0:T(8,128)(2,1)} %ev_hbm.1), custom_call_target="tpu_custom_call" | custom-call | tf_op jit(solution)/shard_map/pallas_call | solution.py:386
  50.5 0.6 %copy.7 = bf16[1,16,16,128]{3,2,1,0:T(8,128)(2,1)} copy(bf16[1,16,16,128]{3,2,1,0:T(8,128)(2,1)S(1)} %bitcast.4) | data formatting | bytes 131072

commit v5 on v4

--- a/solution.py
+++ b/solution.py
@@ -122,31 +122,28 @@
     for dx in x_peers:
         pl.semaphore_signal(known, inc=1, device_id=dev(dx=dx), device_id_type=MESH)
 
-    for dz in (3, 5, 1, 7):
-        at = (n1s[dz], zl0s[1], slice(None), x, nhs[dz], slice(None))
-        pltpu.make_async_remote_copy(
-            aux_n.at[at], q_aux.at[zl // 2, zh], sq.at[0], rq2, device_id=dev(dz=dz), device_id_type=MESH).start()
-        pltpu.make_async_remote_copy(
-            coef.at[at], q_co.at[zl // 2, zh], sq.at[1], rq, device_id=dev(dz=dz), device_id_type=MESH).start()
+    for p in (1, 0):
+        for dz in (3, 5, 1, 7) if p else (4, 2, 6, 0):
+            at = (n1s[dz], zl0s[p], slice(None), x, nhs[dz], slice(None))
+            for src, dst, ssem, rsem in ((aux_n, q_aux, sq.at[0], rq2.at[p]), (coef, q_co, sq.at[1], rq.at[p])):
+                if dz == 0:
+                    pltpu.make_async_copy(src.at[at], dst.at[p, zl // 2, zh], rsem).start()
+                else:
+                    pltpu.make_async_remote_copy(
+                        src.at[at], dst.at[p, zl // 2, zh], ssem, rsem, device_id=dev(dz=dz), device_id_type=MESH).start()
 
     me_yc = y * 2 + c
-    groups = (2, 3, 1, 0)
+    groups = (2, 3, 1)
     own_aux, own_co = [], {}
-
-    def part(g):
-        return slice(None) if g < 3 else zl0s[0]
-
-    def parities(g):
-        return (1, 0) if g < 3 else (0,)
 
     for g, dx in enumerate(groups):
         for dy, dc in yc_peers:
             pltpu.make_async_remote_copy(
-                aux_n.at[:, part(g), ys[dy], xs[dx], :, cs[dc]], a_aux.at[g, :, part(g), :, :, pl.ds(me_yc, 1)], sa.at[0], ra2.at[g],
+                aux_n.at[:, :, ys[dy], xs[dx], :, cs[dc]], a_aux.at[g, :, :, :, :, pl.ds(me_yc, 1)], sa.at[0], ra2.at[g],
                 device_id=dev(dy=dy, dc=dc), device_id_type=MESH).start()
-        own_aux.append(pltpu.make_async_copy(aux_n.at[:, part(g), y, xs[dx], :, c], a_aux.at[g, :, part(g), :, :, pl.ds(me_yc, 1)], lb.at[g]))
+        own_aux.append(pltpu.make_async_copy(aux_n.at[:, :, y, xs[dx], :, c], a_aux.at[g, :, :, :, :, pl.ds(me_yc, 1)], lb.at[g]))
         own_aux[-1].start()
-        for p in parities(g):
+        for p in (1, 0):
             k = g * 2 + 1 - p
             for dy, dc in yc_peers:
                 pltpu.make_async_remote_copy(
@@ -222,15 +219,16 @@
             return [a_co[k, b].reshape(4, 16, 128) for b in range(8)]
         return load
 
+    own_qa, own_q = {}, {}
     for g, dx in enumerate(groups):
         own_aux[g].wait()
-        recv(aux.at[pl.ds(0, 56 if g < 3 else 28)], ra2.at[g])
-        for i in range(8) if g < 3 else range(4):
-            n1, n0, nh = (i // 4, i // 2 % 2, i % 2) if g < 3 else (i // 2, zl0s[0], i % 2)
+        recv(aux.at[pl.ds(0, 56)], ra2.at[g])
+        for i in range(8):
+            n1, n0, nh = i // 4, i // 2 % 2, i % 2
             pack(a_aux[g, n1, n0, nh, 1], a_aux[g, n1, n0, nh, 2], p_send, (g, n1, n0, nh))
-        for dz in (4, 3, 5, 2, 6, 1, 7, 0) if g < 3 else (4, 2, 6, 0):
+        for dz in (4, 3, 5, 2, 6, 1, 7, 0):
             pass_on(dx, dz, p_send.at[g, n1s[dz], zl0s[dz % 2], nhs[dz]], b_aux, sb2, rb2.at[g])
-        for p in parities(g):
+        for p in (1, 0):
             k = g * 2 + 1 - p
             cur = early_levels([a_aux[g, n // 2, zl0s[p], n % 2, 0] for n in range(4)], chunk_of(k, own_co[k]))
             for b in range(8):
@@ -238,31 +236,34 @@
             pass_chunk(k, dx, p, 0)
             if g < 2:
                 pass_chunk(k, dx, p, 1)
-        if g == 0:
-            recv(q_aux, rq2)
-            recv(q_co, rq)
+        if g < 2:
+            q = 1 - g
+            recv(q_aux.at[q], rq2.at[q])
+            recv(q_co.at[q], rq.at[q])
             for dy, dc in yc_peers:
                 to = dev(dy=dy, dc=dc)
                 pltpu.make_async_remote_copy(
-                    q_aux.at[:, :, ys[dy], cs[dc]], qa.at[:, :, :, pl.ds(me_yc, 1)], sqa, rqa, device_id=to, device_id_type=MESH).start()
+                    q_aux.at[q, :, :, ys[dy], cs[dc]], qa.at[q, :, :, :, pl.ds(me_yc, 1)], sqa, rqa.at[q],
+                    device_id=to, device_id_type=MESH).start()
                 pltpu.make_async_remote_copy(
-                    q_co.at[:, :, ys[dy], cs[dc]], a_co.at[6, me_yc], sa.at[1], ra.at[6], device_id=to, device_id_type=MESH).start()
-            own_qa = pltpu.make_async_copy(q_aux.at[:, :, y, c], qa.at[:, :, :, pl.ds(me_yc, 1)], loc.at[8])
-            own_qa.start()
-            own_q = pltpu.make_async_copy(q_co.at[:, :, y, c], a_co.at[6, me_yc], loc.at[6])
-            own_q.start()
+                    q_co.at[q, :, :, ys[dy], cs[dc]], a_co.at[7 - q, me_yc], sa.at[1], ra.at[7 - q],
+                    device_id=to, device_id_type=MESH).start()
+            own_qa[q] = pltpu.make_async_copy(q_aux.at[q, :, :, y, c], qa.at[q, :, :, :, pl.ds(me_yc, 1)], loc.at[8 + q])
+            own_qa[q].start()
+            own_q[q] = pltpu.make_async_copy(q_co.at[q, :, :, y, c], a_co.at[7 - q, me_yc], loc.at[7 - q])
+            own_q[q].start()
 
     pass_chunk(4, 1, 1, 1)
     pass_chunk(5, 1, 0, 1)
-    pass_chunk(7, 0, 0, 1)
-    own_qa.wait()
-    recv(aux.at[pl.ds(0, 28)], rqa)
-    for i in range(4):
-        pack(qa[i // 2, i % 2, 1], qa[i // 2, i % 2, 2], b_aux, (x1, x0, i % 2, i // 2, zl0s[1]))
-    cur = early_levels([qa[n // 2, n % 2, 0] for n in range(4)], chunk_of(6, own_q))
-    for n in range(4):
-        for b in range(8):
-            b_co[x1, x0, n % 2, n // 2, zl0s[1], b // 4, b % 4] = cur[b][n]
+    for q in (1, 0):
+        own_qa[q].wait()
+        recv(aux.at[pl.ds(0, 28)], rqa.at[q])
+        for i in range(4):
+            pack(qa[q, i // 2, i % 2, 1], qa[q, i // 2, i % 2, 2], b_aux, (x1, x0, i % 2, i // 2, zl0s[q]))
+        cur = early_levels([qa[q, n // 2, n % 2, 0] for n in range(4)], chunk_of(7 - q, own_q[q]))
+        for n in range(4):
+            for b in range(8):
+                b_co[x1, x0, n % 2, n // 2, zl0s[q], b // 4, b % 4] = cur[b][n]
 
     def place(dim, bit, fixed_at):
         at = [slice(None)] * 5
@@ -329,11 +330,11 @@
         step_in_place(6, 3, {0: far, 1: b})
 
     near = 1 - x0
+    late_tables(x1, x0)
+    step_in_place(3, 2, {0: x1, 1: x0})
+    step_in_place(4, 4, {0: x1, 1: x0})
     recv(b_aux.at[x1, near], rb2.at[2])
     late_tables(x1, near)
-    recv(b_aux.at[x1, x0, :, :, zl0s[0]], rb2.at[3])
-    late_tables(x1, x0)
-    step_in_place(3, 2, {0: x1, 1: x0, 4: zl0s[1]})
     ev_w = ev[...]
     mine = x * 4 + nhs[0] * 2 + c
     for hf in range(2):
@@ -341,9 +342,6 @@
             recv(b_co.at[x1, near, :, :, zl0s[1 - h], hf], rb.at[4 + h, hf])
             step_in_place(3, 2, {0: x1, 1: near, 4: zl0s[1 - h]}, hf)
         step_in_place(4, 4, {0: x1, 1: near}, hf)
-        recv(b_co.at[x1, x0, :, :, zl0s[0], hf], rb.at[7, hf])
-        step_in_place(3, 2, {0: x1, 1: x0, 4: zl0s[0]}, hf)
-        step_in_place(4, 4, {0: x1, 1: x0}, hf)
         step_in_place(5, 1, {0: x1}, hf)
         step_in_place(6, 3, {0: x1}, hf)
         sums = [[o.reshape(2, 4, 2, 2, 16, 128).sum(axis=(1, 2)) for o in step(7, 0, {1: q}, hf)] for q in range(2)]
@@ -365,13 +363,13 @@
                     pltpu.make_async_remote_copy(
                         osend.at[xs[dx] // 2, xs[dx] % 2, zhs[dh], cs[dc]], out.at[mine], so, ro,
                         device_id=to, device_id_type=MESH).start()
-    recv(b_aux.reshape(32, 3, 4, 128).at[pl.ds(0, 27)], sb2, True)
-    recv(b_co.reshape(32, 8, 16, 128).at[pl.ds(0, 27)], sb, True)
-    recv(aux.at[pl.ds(0, 196)], sa.at[0], True)
+    recv(b_aux.reshape(32, 3, 4, 128).at[pl.ds(0, 24)], sb2, True)
+    recv(b_send.at[pl.ds(0, 6)], sb, True)
+    recv(aux.at[pl.ds(0, 168)], sa.at[0], True)
     recv(a_co.at[pl.ds(0, 7)], sa.at[1], True)
-    recv(q_aux, sq.at[0], True)
-    recv(q_co, sq.at[1], True)
-    recv(aux.at[pl.ds(0, 28)], sqa, True)
+    recv(aux.at[pl.ds(0, 56)], sq.at[0], True)
+    recv(q_co.reshape(8, 4, 2, 16, 128).at[pl.ds(0, 7)], sq.at[1], True)
+    recv(aux.at[pl.ds(0, 56)], sqa, True)
     recv(out, so, True)
     recv(out, ro)
 
@@ -400,18 +398,18 @@
             pltpu.VMEM((8, 4, 8, 16, 128), bf),
             pltpu.VMEM((2, 2, 2, 2, 2, 2, 4, 16, 128), bf),
             pltpu.VMEM((2, 2, 2, 2, 2, 3, 4, 128), i32),
-            pltpu.VMEM((2, 2, 4, 2, 16, 128), bf),
-            pltpu.VMEM((2, 2, 4, 2, 3, 1, 128), i32),
-            pltpu.VMEM((2, 2, 3, 8, 128), i32),
+            pltpu.VMEM((2, 2, 2, 4, 2, 16, 128), bf),
+            pltpu.VMEM((2, 2, 2, 4, 2, 3, 1, 128), i32),
+            pltpu.VMEM((2, 2, 2, 3, 8, 128), i32),
             pltpu.VMEM((3, 2, 4, 8, 128), f32),
             pltpu.VMEM((3, 4, 8, 128), f32),
             pltpu.VMEM((5, 2, 2, 2, 2, 2, 2, 8, 128), f32),
             pltpu.VMEM((5, 2, 2, 2, 2, 2, 8, 128), f32),
             pltpu.VMEM((2, 2, 2, 2, 16, 128), f32),
             pltpu.VMEM((2, 2, 2, 2, 16, 128), bf),
-            dma((4,)), dma((9,)), dma((2,)), dma((8,)), dma((4,)),
+            dma((4,)), dma((10,)), dma((2,)), dma((8,)), dma((4,)),
             dma, dma((8, 2)), dma, dma((4,)), dma, dma, dma((4,)),
-            pltpu.SemaphoreType.REGULAR, dma((2,)), dma, dma, dma, dma,
+            pltpu.SemaphoreType.REGULAR, dma((2,)), dma((2,)), dma((2,)), dma, dma((2,)),
         ],
         compiler_params=pltpu.CompilerParams(
             collective_id=0, has_side_effects=True, vmem_limit_bytes=66912256),

time: 51.2 us -> 50.1 us (0.979)
  Pallas kernels: 50.5 us -> 49.4 us
    pallas_call x1, Pallas kernels: 50.5 us -> 49.4 us  [per_device(): pl.pallas_call(kernel, out_shape=pltpu.VMEM((16, 16, 128), bf), in_specs=...]
where the time goes in v5:
time: 50.1 us; the launch traced here: 50 us
  Pallas kernels  49.4 us (99%)
  local copies, waits for them, and re-layouts  0.63 us (1%)
    pallas_call x1, Pallas kernels, per_device(): pl.pallas_call(kernel, out_shape=pltpu.VMEM((16, 16, 128), bf), in_specs=...  49.4 us

profile of v5, /device:TPU:1, one launch (start us, length us, event | category | flops | bytes accessed | tf_op | source)
XLA Modules:
  0.0 50.0 jit_solution(5282663571990402737)
XLA Ops:
  0.0 49.4 %shard_map.55 = bf16[16,16,128]{2,1,0:T(8,128)(2,1)S(1)} custom-call(bf16[2,2,4,4,2,2,16,128]{7,6,5,4,3,2,1,0:T(8,128)(2,1)} %bitcast.6, f32[8,64,256]{2,1,0:T(8,128)} %bitcast.7, s32[8,256]{1,0:T(8,128)} %cls_hbm.1, bf16[8,512,256]{2,1,0:T(8,128)(2,1)} %bitcast.5, bf16[128,128]{1,0:T(8,128)(2,1)} %ev_hbm.1), custom_call_target="tpu_custom_call" | custom-call | tf_op jit(solution)/shard_map/pallas_call | solution.py:384
  49.4 0.6 %copy.7 = bf16[1,16,16,128]{3,2,1,0:T(8,128)(2,1)} copy(bf16[1,16,16,128]{3,2,1,0:T(8,128)(2,1)S(1)} %bitcast.4) | data formatting | bytes 131072

commit v6 on v5

--- a/solution.py
+++ b/solution.py
@@ -122,7 +122,7 @@
     for dx in x_peers:
         pl.semaphore_signal(known, inc=1, device_id=dev(dx=dx), device_id_type=MESH)
 
-    for p in (1, 0):
+    def along_z(p):
         for dz in (3, 5, 1, 7) if p else (4, 2, 6, 0):
             at = (n1s[dz], zl0s[p], slice(None), x, nhs[dz], slice(None))
             for src, dst, ssem, rsem in ((aux_n, q_aux, sq.at[0], rq2.at[p]), (coef, q_co, sq.at[1], rq.at[p])):
@@ -131,6 +131,8 @@
                 else:
                     pltpu.make_async_remote_copy(
                         src.at[at], dst.at[p, zl // 2, zh], ssem, rsem, device_id=dev(dz=dz), device_id_type=MESH).start()
+
+    along_z(1)
 
     me_yc = y * 2 + c
     groups = (2, 3, 1)
@@ -151,6 +153,8 @@
                     device_id=dev(dy=dy, dc=dc), device_id_type=MESH).start()
             own_co[k] = pltpu.make_async_copy(coef.at[:, zl0s[p], y, xs[dx], :, c], a_co.at[k, me_yc], loc.at[k])
             own_co[k].start()
+        if g == 0:
+            along_z(0)
     copies[2].wait()
     copies[3].wait()
 

time: 50.1 us -> 50.1 us (level)
  no operation moved by 1% of the time
where the time goes in v6:
time: 50.1 us; the launch traced here: 50 us
  Pallas kernels  49.4 us (99%)
  local copies, waits for them, and re-layouts  0.63 us (1%)
    pallas_call x1, Pallas kernels, per_device(): pl.pallas_call(kernel, out_shape=pltpu.VMEM((16, 16, 128), bf), in_specs=...  49.4 us

profile of v6, /device:TPU:1, one launch (start us, length us, event | category | flops | bytes accessed | tf_op | source)
XLA Modules:
  0.0 50.0 jit_solution(3933521765235148064)
XLA Ops:
  0.0 49.4 %shard_map.55 = bf16[16,16,128]{2,1,0:T(8,128)(2,1)S(1)} custom-call(bf16[2,2,4,4,2,2,16,128]{7,6,5,4,3,2,1,0:T(8,128)(2,1)} %bitcast.6, f32[8,64,256]{2,1,0:T(8,128)} %bitcast.7, s32[8,256]{1,0:T(8,128)} %cls_hbm.1, bf16[8,512,256]{2,1,0:T(8,128)(2,1)} %bitcast.5, bf16[128,128]{1,0:T(8,128)(2,1)} %ev_hbm.1), custom_call_target="tpu_custom_call" | custom-call | tf_op jit(solution)/shard_map/pallas_call | solution.py:388
  49.4 0.6 %copy.7 = bf16[1,16,16,128]{3,2,1,0:T(8,128)(2,1)} copy(bf16[1,16,16,128]{3,2,1,0:T(8,128)(2,1)S(1)} %bitcast.4) | data formatting | bytes 131072
